TPU v7x, 32 devices: a whole 2x2x4 slice. The times are simulated.
32 devices in a mesh: shard: 8 (over z, x), tensor: 4 (over y, core).
Axes of the slice: x: 2, y: 2, z: 4, core: 2. Of those that a mesh axis runs over, the one named last changes fastest.
Arguments:
- tokens: bfloat16 [8192, 1024], P('shard'), may hold values from -6 to 6
- cotangent: bfloat16 [8192, 1024], P('shard'), may hold values from -6 to 6
- ln_gain: bfloat16 [2, 2, 1024], P(None, None, 'shard'), may hold values from 0.25 to 1.75
- ln_bias: bfloat16 [2, 2, 1024], P(None, None, 'shard'), may hold values from -1.75 to 1.75
- w_qkv: bfloat16 [2, 1024, 3072], P(None, 'shard', 'tensor'), may hold values from -0.25 to 0.25
- b_qkv: bfloat16 [2, 3072], P(None, ('tensor', 'shard')), may hold values from -1.75 to 1.75
- w_dense: bfloat16 [2, 1024, 1024], P(None, 'tensor', 'shard'), may hold values from -0.5 to 0.5
- b_dense: bfloat16 [2, 1024], P(None, 'shard'), may hold values from -1.75 to 1.75
- w_fc1: bfloat16 [2, 1024, 4096], P(None, 'shard', 'tensor'), may hold values from -0.1875 to 0.1875
- b_fc1: bfloat16 [2, 4096], P(None, ('tensor', 'shard')), may hold values from -1.75 to 1.75
- w_fc2: bfloat16 [2, 4096, 1024], P(None, 'tensor', 'shard'), may hold values from -0.125 to 0.125
- b_fc2: bfloat16 [2, 1024], P(None, 'shard'), may hold values from -1.75 to 1.75
Outputs:
- output: bfloat16 [8192, 1024], P('shard')
- d_tokens: bfloat16 [8192, 1024], P('shard')
- d_ln_gain: float32 [2, 2, 1024], P(None, None, 'shard')
- d_ln_bias: float32 [2, 2, 1024], P(None, None, 'shard')
- d_w_qkv: float32 [2, 1024, 3072], P(None, 'shard', 'tensor')
- d_b_qkv: float32 [2, 3072], P(None, ('tensor', 'shard'))
- d_w_dense: float32 [2, 1024, 1024], P(None, 'tensor', 'shard')
- d_b_dense: float32 [2, 1024], P(None, 'shard')
- d_w_fc1: float32 [2, 1024, 4096], P(None, 'shard', 'tensor')
- d_b_fc1: float32 [2, 4096], P(None, ('tensor', 'shard'))
- d_w_fc2: float32 [2, 4096, 1024], P(None, 'tensor', 'shard')
- d_b_fc2: float32 [2, 1024], P(None, 'shard')
All inputs are finite; a program needn't handle non-finite values.
Results may differ from a plain program's by a relative error of at most 0.04.
Values may be sent and summed in bfloat16 or wider, within the bound.
No kernel may reach another device: no remote copies, remote signals or barrier semaphores. Data moves between devices by JAX's collectives and lax.ppermute only.
A program may use at most 192 MiB of HBM per device.

v0:
```python
import math

import jax
import jax.numpy as jnp
from jax import lax
from jax.sharding import PartitionSpec as P

HD = 64
ROT = 16
LAYERS = 2
LEN = 512


def rotate_tables(token_count):
    half = ROT // 2
    places = (jnp.arange(token_count) % LEN).astype(jnp.float32)
    freqs = jnp.exp(-(2.0 * jnp.arange(half).astype(jnp.float32) / ROT) * math.log(10000.0))
    angles = places[:, None] * freqs[None, :]
    angles = jnp.concatenate([angles, angles], axis=1)
    return (jnp.cos(angles)[:, None, :], jnp.sin(angles)[:, None, :])


def rotate(part, cosine, sine):
    inner = part[..., :ROT]
    lower = inner[..., : ROT // 2]
    upper = inner[..., ROT // 2 :]
    turned = inner * cosine + jnp.concatenate([-upper, lower], axis=-1) * sine
    return jnp.concatenate([turned, part[..., ROT:]], axis=-1)


def rotate_back(grad, cosine, sine):
    inner = grad[..., :ROT]
    scaled = inner * sine
    lower = scaled[..., : ROT // 2]
    upper = scaled[..., ROT // 2 :]
    turned = inner * cosine + jnp.concatenate([upper, -lower], axis=-1)
    return jnp.concatenate([turned, grad[..., ROT:]], axis=-1)


def normalize(resid):
    centered = resid - jnp.mean(resid, axis=-1, keepdims=True)
    factor = lax.rsqrt(jnp.mean(centered * centered, axis=-1, keepdims=True) + 1e-05)
    return (centered * factor, factor)


def norm_input(grad, normed, factor, gain_row):
    shaped = grad * gain_row
    return factor * (
        shaped
        - jnp.mean(shaped, axis=-1, keepdims=True)
        - normed * jnp.mean(shaped * normed, axis=-1, keepdims=True)
    )


def norm_parts(d_first, d_second, normed, factor, gains):
    d_input = norm_input(d_first, normed, factor, gains[0]) + norm_input(
        d_second, normed, factor, gains[1]
    )
    d_gain = jnp.stack([jnp.sum(d_first * normed, axis=0), jnp.sum(d_second * normed, axis=0)])
    d_shift = jnp.stack([jnp.sum(d_first, axis=0), jnp.sum(d_second, axis=0)])
    return (d_input, d_gain, d_shift)


def gelu_slope(hidden_in):
    normal_cdf = 0.5 * (1.0 + jax.scipy.special.erf(hidden_in * (1.0 / math.sqrt(2.0))))
    density = jnp.exp(-0.5 * hidden_in * hidden_in) * (1.0 / math.sqrt(2.0 * math.pi))
    return normal_cdf + hidden_in * density


def attention_scores(queries, key_rows, causal):
    scores = jnp.einsum("bqhd,bkhd->bhqk", queries, key_rows, preferred_element_type=jnp.float32)
    scores = scores * (1.0 / math.sqrt(HD))
    return jnp.where(causal, scores, -1e30)


def per_device(
    tokens, cotangent, ln_gain, ln_bias, w_qkv, b_qkv, w_dense, b_dense, w_fc1, b_fc1, w_fc2, b_fc2
):
    token_count = tokens.shape[0]
    seq_count = token_count // LEN
    cosine, sine = rotate_tables(token_count)
    causal = jnp.arange(LEN)[:, None] >= jnp.arange(LEN)[None, :]
    resid = tokens.astype(jnp.float32)
    stored = []
    for layer in range(LAYERS):
        weights = (
            lax.all_gather(ln_gain[layer], "shard", axis=1, tiled=True),
            lax.all_gather(ln_bias[layer], "shard", axis=1, tiled=True),
            lax.all_gather(w_qkv[layer], "shard", axis=0, tiled=True),
            lax.all_gather(b_qkv[layer], "shard", axis=0, tiled=True),
            lax.all_gather(w_dense[layer], "shard", axis=1, tiled=True),
            lax.all_gather(b_dense[layer], "shard", axis=0, tiled=True),
            lax.all_gather(w_fc1[layer], "shard", axis=0, tiled=True),
            lax.all_gather(b_fc1[layer], "shard", axis=0, tiled=True),
            lax.all_gather(w_fc2[layer], "shard", axis=1, tiled=True),
            lax.all_gather(b_fc2[layer], "shard", axis=0, tiled=True),
        )
        (
            gains,
            shifts,
            qkv_mat,
            qkv_bias,
            dense_mat,
            dense_bias,
            up_mat,
            up_bias,
            down_mat,
            down_bias,
        ) = weights
        gains = gains.astype(jnp.float32)
        shifts = shifts.astype(jnp.float32)
        normed, factor = normalize(resid)
        first = (normed * gains[0] + shifts[0]).astype(jnp.bfloat16)
        second = (normed * gains[1] + shifts[1]).astype(jnp.bfloat16)
        head_count = qkv_mat.shape[1] // (3 * HD)
        joined = jnp.dot(first, qkv_mat, preferred_element_type=jnp.float32) + qkv_bias.astype(
            jnp.float32
        )
        joined = joined.reshape(token_count, head_count, 3, HD)
        queries = (
            rotate(joined[:, :, 0], cosine, sine)
            .astype(jnp.bfloat16)
            .reshape(seq_count, LEN, head_count, HD)
        )
        key_rows = (
            rotate(joined[:, :, 1], cosine, sine)
            .astype(jnp.bfloat16)
            .reshape(seq_count, LEN, head_count, HD)
        )
        value_rows = joined[:, :, 2].astype(jnp.bfloat16).reshape(seq_count, LEN, head_count, HD)
        scores = attention_scores(queries, key_rows, causal)
        highest = jnp.max(scores, axis=-1, keepdims=True)
        log_total = highest + jnp.log(jnp.sum(jnp.exp(scores - highest), axis=-1, keepdims=True))
        chances = jnp.exp(scores - log_total).astype(jnp.bfloat16)
        mixed = jnp.einsum(
            "bhqk,bkhd->bqhd", chances, value_rows, preferred_element_type=jnp.float32
        )
        mixed = mixed.astype(jnp.bfloat16).reshape(token_count, head_count * HD)
        hidden_in = jnp.dot(second, up_mat, preferred_element_type=jnp.float32) + up_bias.astype(
            jnp.float32
        )
        hidden = jax.nn.gelu(hidden_in, approximate=False).astype(jnp.bfloat16)
        partial_branch = jnp.dot(mixed, dense_mat, preferred_element_type=jnp.float32) + jnp.dot(
            hidden, down_mat, preferred_element_type=jnp.float32
        )
        branch = lax.psum(partial_branch.astype(jnp.bfloat16), "tensor").astype(jnp.float32)
        branch = branch + dense_bias.astype(jnp.float32) + down_bias.astype(jnp.float32)
        stored.append(
            (
                normed,
                factor,
                first,
                second,
                queries,
                key_rows,
                value_rows,
                log_total,
                mixed,
                hidden_in,
                hidden,
                weights,
            )
        )
        resid = resid + branch
    output = resid.astype(jnp.bfloat16)
    grad = cotangent.astype(jnp.float32)
    results = [None] * LAYERS
    for layer in reversed(range(LAYERS)):
        (
            normed,
            factor,
            first,
            second,
            queries,
            key_rows,
            value_rows,
            log_total,
            mixed,
            hidden_in,
            hidden,
            weights,
        ) = stored[layer]
        weights = (
            lax.all_gather(ln_gain[layer], "shard", axis=1, tiled=True),
            lax.all_gather(ln_bias[layer], "shard", axis=1, tiled=True),
            lax.all_gather(w_qkv[layer], "shard", axis=0, tiled=True),
            lax.all_gather(b_qkv[layer], "shard", axis=0, tiled=True),
            lax.all_gather(w_dense[layer], "shard", axis=1, tiled=True),
            lax.all_gather(b_dense[layer], "shard", axis=0, tiled=True),
            lax.all_gather(w_fc1[layer], "shard", axis=0, tiled=True),
            lax.all_gather(b_fc1[layer], "shard", axis=0, tiled=True),
            lax.all_gather(w_fc2[layer], "shard", axis=1, tiled=True),
            lax.all_gather(b_fc2[layer], "shard", axis=0, tiled=True),
        )
        (
            gains,
            shifts,
            qkv_mat,
            qkv_bias,
            dense_mat,
            dense_bias,
            up_mat,
            up_bias,
            down_mat,
            down_bias,
        ) = weights
        gains = gains.astype(jnp.float32)
        head_count = qkv_mat.shape[1] // (3 * HD)
        grad_low = grad.astype(jnp.bfloat16)
        d_out_bias = jnp.sum(grad_low.astype(jnp.float32), axis=0)
        d_dense = jnp.einsum("td,te->de", mixed, grad_low, preferred_element_type=jnp.float32)
        d_down = jnp.einsum("tf,te->fe", hidden, grad_low, preferred_element_type=jnp.float32)
        d_mixed = jnp.einsum("te,de->td", grad_low, dense_mat, preferred_element_type=jnp.float32)
        d_mixed = d_mixed.astype(jnp.bfloat16).reshape(seq_count, LEN, head_count, HD)
        d_hidden = jnp.einsum("te,fe->tf", grad_low, down_mat, preferred_element_type=jnp.float32)
        d_hidden_in = (d_hidden * gelu_slope(hidden_in)).astype(jnp.bfloat16)
        d_up_bias = jnp.sum(d_hidden_in.astype(jnp.float32), axis=0)
        d_up = jnp.einsum("td,tf->df", second, d_hidden_in, preferred_element_type=jnp.float32)
        d_second = jnp.einsum("tf,df->td", d_hidden_in, up_mat, preferred_element_type=jnp.float32)
        scores = attention_scores(queries, key_rows, causal)
        chances = jnp.exp(scores - log_total)
        d_value = jnp.einsum(
            "bhqk,bqhd->bkhd",
            chances.astype(jnp.bfloat16),
            d_mixed,
            preferred_element_type=jnp.float32,
        )
        d_chances = jnp.einsum(
            "bqhd,bkhd->bhqk", d_mixed, value_rows, preferred_element_type=jnp.float32
        )
        row_inner = jnp.sum(chances * d_chances, axis=-1, keepdims=True)
        d_scores = (chances * (d_chances - row_inner)).astype(jnp.bfloat16)
        d_query = jnp.einsum(
            "bhqk,bkhd->bqhd", d_scores, key_rows, preferred_element_type=jnp.float32
        ) * (1.0 / math.sqrt(HD))
        d_key = jnp.einsum(
            "bhqk,bqhd->bkhd", d_scores, queries, preferred_element_type=jnp.float32
        ) * (1.0 / math.sqrt(HD))
        d_joined = jnp.stack(
            [
                rotate_back(d_query.reshape(token_count, head_count, HD), cosine, sine),
                rotate_back(d_key.reshape(token_count, head_count, HD), cosine, sine),
                d_value.reshape(token_count, head_count, HD),
            ],
            axis=2,
        )
        d_joined = d_joined.astype(jnp.bfloat16).reshape(token_count, head_count * 3 * HD)
        d_qkv_bias = jnp.sum(d_joined.astype(jnp.float32), axis=0)
        d_qkv = jnp.einsum("td,tc->dc", first, d_joined, preferred_element_type=jnp.float32)
        d_first = jnp.einsum("tc,dc->td", d_joined, qkv_mat, preferred_element_type=jnp.float32)
        d_first, d_second = (
            lax.psum(d_first.astype(jnp.bfloat16), "tensor").astype(jnp.float32),
            lax.psum(d_second.astype(jnp.bfloat16), "tensor").astype(jnp.float32),
        )
        d_input, d_gain, d_shift = norm_parts(d_first, d_second, normed, factor, gains)
        grad = grad + d_input
        results[layer] = (
            lax.psum_scatter(
                d_gain.astype(jnp.bfloat16), "shard", scatter_dimension=1, tiled=True
            ).astype(jnp.float32),
            lax.psum_scatter(
                d_shift.astype(jnp.bfloat16), "shard", scatter_dimension=1, tiled=True
            ).astype(jnp.float32),
            lax.psum_scatter(
                d_qkv.astype(jnp.bfloat16), "shard", scatter_dimension=0, tiled=True
            ).astype(jnp.float32),
            lax.psum_scatter(
                d_qkv_bias.astype(jnp.bfloat16), "shard", scatter_dimension=0, tiled=True
            ).astype(jnp.float32),
            lax.psum_scatter(
                d_dense.astype(jnp.bfloat16), "shard", scatter_dimension=1, tiled=True
            ).astype(jnp.float32),
            lax.psum_scatter(
                d_out_bias.astype(jnp.bfloat16), "shard", scatter_dimension=0, tiled=True
            ).astype(jnp.float32),
            lax.psum_scatter(
                d_up.astype(jnp.bfloat16), "shard", scatter_dimension=0, tiled=True
            ).astype(jnp.float32),
            lax.psum_scatter(
                d_up_bias.astype(jnp.bfloat16), "shard", scatter_dimension=0, tiled=True
            ).astype(jnp.float32),
            lax.psum_scatter(
                d_down.astype(jnp.bfloat16), "shard", scatter_dimension=1, tiled=True
            ).astype(jnp.float32),
        )

    def stacked(index):
        return jnp.stack([results[layer][index] for layer in range(LAYERS)])

    return (
        output,
        grad.astype(jnp.bfloat16),
        stacked(0),
        stacked(1),
        stacked(2),
        stacked(3),
        stacked(4),
        stacked(5),
        stacked(6),
        stacked(7),
        stacked(8),
        stacked(5),
    )


def solution(mesh):
    in_specs = (
        P("shard", None),
        P("shard", None),
        P(None, None, "shard"),
        P(None, None, "shard"),
        P(None, "shard", "tensor"),
        P(None, ("tensor", "shard")),
        P(None, "tensor", "shard"),
        P(None, "shard"),
        P(None, "shard", "tensor"),
        P(None, ("tensor", "shard")),
        P(None, "tensor", "shard"),
        P(None, "shard"),
    )
    out_specs = (
        P("shard", None),
        P("shard", None),
        P(None, None, "shard"),
        P(None, None, "shard"),
        P(None, "shard", "tensor"),
        P(None, ("tensor", "shard")),
        P(None, "tensor", "shard"),
        P(None, "shard"),
        P(None, "shard", "tensor"),
        P(None, ("tensor", "shard")),
        P(None, "tensor", "shard"),
        P(None, "shard"),
    )
    return jax.shard_map(
        per_device, mesh=mesh, in_specs=in_specs, out_specs=out_specs, check_vma=False
    )
```

profile of v0, /device:TPU:0, one launch (start us, length us, event | category | flops | bytes accessed | tf_op | source)
XLA Modules:
  0.0 1468.3 jit_solution(8617966456069188106)
XLA Ops:
  19.1 22.3 %all-gather.6 = bf16[1,1024]{1,0:T(2,128)(2,1)S(1)} all-gather(bf16[1,128]{1,0:T(2,128)(2,1)S(1)} %get-tuple-element.114), channel_id=8, replica_groups=mesh['shard'=8,'tensor'=4] {'shard'}, dimensions={1}, use_global_device_ids=true | all-gather | bytes 2304 | tf_op jit(solution)/shard_map/all_gather | solution.py:94
  42.0 16.5 %all-gather.1 = bf16[1,2,1024]{2,1,0:T(2,128)(2,1)S(1)} all-gather(bf16[1,2,128]{2,1,0:T(2,128)(2,1)S(1)} %get-tuple-element.105), channel_id=3, replica_groups=mesh['shard'=8,'tensor'=4] {'shard'}, dimensions={2}, use_global_device_ids=true | all-gather | bytes 4608 | tf_op jit(solution)/shard_map/all_gather | solution.py:88
  59.1 18.3 %all-gather = bf16[1,2,1024]{2,1,0:T(2,128)(2,1)S(1)} all-gather(bf16[1,2,128]{2,1,0:T(2,128)(2,1)S(1)} %get-tuple-element.103), channel_id=2, replica_groups=mesh['shard'=8,'tensor'=4] {'shard'}, dimensions={2}, use_global_device_ids=true | all-gather | bytes 4608 | tf_op jit(solution)/shard_map/all_gather | solution.py:87
  80.8 18.3 %all-reduce.9 = (bf16[768]{0:T(1024)(128)(2,1)S(1)}, bf16[768]{0:T(1024)(128)(2,1)}) all-reduce(bf16[768]{0:T(1024)(128)(2,1)S(1)} %dynamic-update-slice, bf16[768]{0:T(1024)(128)(2,1)S(1)} %dynamic-update-slice.1), channel_id=5, replica_groups=mesh['shard'=8,'tensor'=4] {'shard'}, use_global_device_ids=true, to_apply=%add | all-reduce | flops 1536 | bytes 6144
  99.3 28.8 %all-gather.4 = bf16[1,256,1024]{2,1,0:T(8,128)(2,1)S(1)} all-gather(bf16[1,256,128]{2,1,0:T(8,128)(2,1)S(1)} %get-tuple-element.80), channel_id=6, replica_groups=mesh['shard'=8,'tensor'=4] {'shard'}, dimensions={2}, use_global_device_ids=true | all-gather | bytes 589824 | tf_op jit(solution)/shard_map/all_gather | solution.py:91
  128.1 3.8 convolution_add_fusion.1
  140.0 5.7 fusion.107
  146.3 14.9 %fusion.48 = (bf16[1024,1024]{1,0:T(8,128)(2,1)}, f32[1024,1024]{1,0:T(8,128)}) fusion(f32[1024]{0:T(1024)} %bitcast.364, bf16[1,1024,1024]{2,1,0:T(8,128)(2,1)} %all-gather.29.cloned.1.call-done, bf16[1024,1024]{1,0:T(8,128)(2,1)S(1)} %copy-done.2, f32[1024]{0:T(1024)} %bitcast.368, f32[1024]{0:T(1024)} %bitcast.354, f32[1024]{0:T(1024)} %copy-done.60, ...), kind=kOutput, calls=%fused_computation.73 | convolution fusion | flops 2222981120 | bytes 10506240 | tf_op jit(solution)/shard_map/dot_general | solution.py:139
  161.2 4.8 all-gather.31.cloned.1.call-done
  165.9 4.5 fusion.86
  174.6 28.1 %all-gather.14 = bf16[1,256,1024]{2,1,0:T(8,128)(2,1)S(1)} all-gather(bf16[1,256,128]{2,1,0:T(8,128)(2,1)} %get-tuple-element.79), channel_id=16, replica_groups=mesh['shard'=8,'tensor'=4] {'shard'}, dimensions={2}, use_global_device_ids=true | all-gather | bytes 589824 | tf_op jit(solution)/shard_map/all_gather | solution.py:91
  203.5 3.3 convolution_convert_fusion.13
  210.2 16.5 %all-gather.11 = bf16[1,2,1024]{2,1,0:T(2,128)(2,1)S(1)} all-gather(bf16[1,2,128]{2,1,0:T(2,128)(2,1)} %get-tuple-element.106), channel_id=13, replica_groups=mesh['shard'=8,'tensor'=4] {'shard'}, dimensions={2}, use_global_device_ids=true | all-gather | bytes 4608 | tf_op jit(solution)/shard_map/all_gather | solution.py:88
  227.3 18.4 %all-gather.10 = bf16[1,2,1024]{2,1,0:T(2,128)(2,1)S(1)} all-gather(bf16[1,2,128]{2,1,0:T(2,128)(2,1)} %get-tuple-element.104), channel_id=12, replica_groups=mesh['shard'=8,'tensor'=4] {'shard'}, dimensions={2}, use_global_device_ids=true | all-gather | bytes 4608 | tf_op jit(solution)/shard_map/all_gather | solution.py:87
  246.8 16.5 %all-gather.9 = bf16[1,1024]{1,0:T(2,128)(2,1)S(1)} all-gather(bf16[1,128]{1,0:T(2,128)(2,1)S(1)} %get-tuple-element.112), channel_id=11, replica_groups=mesh['shard'=8,'tensor'=4] {'shard'}, dimensions={1}, use_global_device_ids=true | all-gather | bytes 2304 | tf_op jit(solution)/shard_map/all_gather | solution.py:96
  263.9 18.3 %all-gather.8 = bf16[1,1024]{1,0:T(2,128)(2,1)S(1)} all-gather(bf16[1,128]{1,0:T(2,128)(2,1)S(1)} %get-tuple-element.110), channel_id=10, replica_groups=mesh['shard'=8,'tensor'=4] {'shard'}, dimensions={1}, use_global_device_ids=true | all-gather | bytes 2304 | tf_op jit(solution)/shard_map/all_gather | solution.py:92
  282.2 16.7 %all-gather.16 = bf16[1,1024]{1,0:T(2,128)(2,1)S(1)} all-gather(bf16[1,128]{1,0:T(2,128)(2,1)S(1)} %copy-done.88), channel_id=18, replica_groups=mesh['shard'=8,'tensor'=4] {'shard'}, dimensions={1}, use_global_device_ids=true | all-gather | bytes 2304 | tf_op jit(solution)/shard_map/all_gather | solution.py:94
  299.5 2.6 fusion.92
  303.5 4.4 convolution_add_fusion
  318.5 2.3 convolution_bitcast_fusion.1
  320.8 3.1 multiply_reduce_fusion.1
  324.0 2.6 multiply_convert_fusion.1
  342.9 3.2 convolution_convert_fusion.5
  346.1 15.1 %fusion.51 = (bf16[1024,1024]{1,0:T(8,128)(2,1)}, f32[1024,1024]{1,0:T(8,128)}) fusion(f32[1024]{0:T(1024)S(1)} %bitcast.366, bf16[1,1024,1024]{2,1,0:T(8,128)(2,1)} %all-gather.35.cloned.1.call-done, f32[1024]{0:T(1024)S(1)} %bitcast.372, f32[1024]{0:T(1024)S(1)} %bitcast.342, f32[1024]{0:T(1024)S(1)} %copy-done.51, f32[1024]{0:T(1024)S(1)} %copy-done.45, ...), kind=kOutput, calls=%fused_computation.76 | convolution fusion | flops 2227175424 | bytes 12611584 | tf_op jit(solution)/shard_map/dot_general | solution.py:139
  361.2 8.6 all-gather.37.cloned.1.call-done
  369.8 7.4 fusion.165
  378.5 3.7 fusion.96
  383.3 6.4 fusion.108
  390.3 2.3 fusion.79
  394.8 71.3 %all-reduce.20.cloned.1.call-done = (bf16[1024,1024]{1,0:T(8,128)(2,1)}, bf16[1024,1024]{1,0:T(8,128)(2,1)}) async-done(((bf16[1024,1024]{1,0:T(8,128)(2,1)}, bf16[1024,1024]{1,0:T(8,128)(2,1)}), (bf16[1024,1024]{1,0:T(8,128)(2,1)}, bf16[1024,1024]{1,0:T(8,128)(2,1)})) %all-reduce.20.cloned.1.call-update) | async-done | bytes 4194320 | tf_op jit(solution)/shard_map/psum | solution.py:252
  466.2 7.8 fusion.38
  474.0 6.5 fusion.141
  486.7 5.8 convolution_bitcast_fusion
  492.6 5.4 multiply_reduce_fusion
  498.0 2.8 multiply_convert_fusion
  514.2 3.2 convolution_convert_fusion.4
  518.9 3.9 fusion.166
  524.1 3.7 fusion.93
  528.9 3.1 convolution_convert_fusion.10
  539.8 6.0 convolution_convert_fusion
  545.8 4.0 copy.147
  550.0 6.2 convolution_convert_fusion.6
  556.3 4.8 convolution_convert_fusion.7
  561.2 86.6 %all-reduce.18.cloned.1.call-done = (bf16[1024,1024]{1,0:T(8,128)(2,1)}, bf16[1024,1024]{1,0:T(8,128)(2,1)}, bf16[1024,1024]{1,0:T(8,128)(2,1)}) async-done(((bf16[1024,1024]{1,0:T(8,128)(2,1)}, bf16[1024,1024]{1,0:T(8,128)(2,1)}, bf16[1024,1024]{1,0:T(8,128)(2,1)}), (bf16[1024,1024]{1,0:T(8,128)(2,1)}, bf16[1024,1024]{1,0:T(8,128)(2,1)}, bf16[1024,1024]{1,0:T(8,128)(2,1)})) %all-reduce.18.cloned.1.call-update) | async-done | bytes 6291472 | tf_op jit(solution)/shard_map/psum | solution.py:146
  647.8 5.7 fusion.43
  659.7 5.9 convolution_convert_fusion.1
  665.7 3.9 copy.145
  669.7 6.6 convolution_convert_fusion.2
  676.4 5.6 convolution_convert_fusion.3
  682.1 20.5 %all-gather.19 = bf16[1,1024]{1,0:T(2,128)(2,1)S(1)} all-gather(bf16[1,128]{1,0:T(2,128)(2,1)S(1)} %copy-done.86), channel_id=21, replica_groups=mesh['shard'=8,'tensor'=4] {'shard'}, dimensions={1}, use_global_device_ids=true | all-gather | bytes 2304 | tf_op jit(solution)/shard_map/all_gather | solution.py:96
  702.6 16.3 %all-gather.18 = bf16[1,1024]{1,0:T(2,128)(2,1)S(1)} all-gather(bf16[1,128]{1,0:T(2,128)(2,1)S(1)} %copy-done.87), channel_id=20, replica_groups=mesh['shard'=8,'tensor'=4] {'shard'}, dimensions={1}, use_global_device_ids=true | all-gather | bytes 2304 | tf_op jit(solution)/shard_map/all_gather | solution.py:92
  721.3 34.9 %all-reduce.8 = (bf16[768]{0:T(1024)(128)(2,1)S(1)}, bf16[768]{0:T(1024)(128)(2,1)S(1)}, bf16[1024]{0:T(1024)(128)(2,1)S(1)}, bf16[1024]{0:T(1024)(128)(2,1)S(1)...) all-reduce(bf16[768]{0:T(1024)(128)(2,1)S(1)} %reduce_sum.319, ...), channel_id=29, replica_groups=mesh['shard'=8,'tensor'=4] {'shard'}, use_global_device_ids=true, to_apply=%region_41.42.clone | all-reduce | flops 5632 | bytes 22528
  757.8 21.7 %reduce-scatter.39.cloned.1.call-done = bf16[128,2]{1,0:T(8,128)(2,1)} async-done(((bf16[1024,2]{1,0:T(8,128)(2,1)}), bf16[128,2]{1,0:T(8,128)(2,1)}) %reduce-scatter.39.cloned.1.call-update) | async-done | bytes 528
  780.3 63.5 %reduce-scatter.43.cloned.1.call-done = bf16[128,2]{1,0:T(8,128)(2,1)} async-done(((bf16[1024,2]{1,0:T(8,128)(2,1)}), bf16[128,2]{1,0:T(8,128)(2,1)}) %reduce-scatter.43.cloned.1.call-update) | async-done | bytes 528
  844.6 64.8 %reduce-scatter.45.cloned.1.call-done = bf16[128,256]{1,0:T(8,128)(2,1)} async-done(((bf16[1024,256]{1,0:T(8,128)(2,1)}), bf16[128,256]{1,0:T(8,128)(2,1)}) %reduce-scatter.45.cloned.1.call-update) | async-done | bytes 65552
  911.1 69.2 %reduce-scatter.51.cloned.1.call-done = bf16[128,1024]{1,0:T(8,128)(2,1)} async-done(((bf16[1024,1024]{1,0:T(8,128)(2,1)}), bf16[128,1024]{1,0:T(8,128)(2,1)}) %reduce-scatter.51.cloned.1.call-update) | async-done | bytes 262160
  981.5 66.8 %reduce-scatter.31.cloned.1.call-done = bf16[128,768]{1,0:T(8,128)(2,1)} async-done(((bf16[1024,768]{1,0:T(8,128)(2,1)}), bf16[128,768]{1,0:T(8,128)(2,1)}) %reduce-scatter.31.cloned.1.call-update) | async-done | bytes 196624 | tf_op jit(solution)/shard_map/reduce_scatter | solution.py:264
  1048.3 67.6 %reduce-scatter.29.cloned.1.call-done = bf16[128,768]{1,0:T(8,128)(2,1)} async-done(((bf16[1024,768]{1,0:T(8,128)(2,1)}), bf16[128,768]{1,0:T(8,128)(2,1)}) %reduce-scatter.29.cloned.1.call-update) | async-done | bytes 196624 | tf_op jit(solution)/shard_map/reduce_scatter | solution.py:264
  1117.9 7.9 fusion.30
  1125.8 54.7 %reduce-scatter.37.cloned.1.call-done = bf16[128,2]{1,0:T(8,128)(2,1)} async-done(((bf16[1024,2]{1,0:T(8,128)(2,1)}), bf16[128,2]{1,0:T(8,128)(2,1)}) %reduce-scatter.37.cloned.1.call-update) | async-done | bytes 528
  1181.4 63.5 %reduce-scatter.41.cloned.1.call-done = bf16[128,2]{1,0:T(8,128)(2,1)} async-done(((bf16[1024,2]{1,0:T(8,128)(2,1)}), bf16[128,2]{1,0:T(8,128)(2,1)}) %reduce-scatter.41.cloned.1.call-update) | async-done | bytes 528
  1246.9 68.9 %reduce-scatter.49.cloned.1.call-done = bf16[128,1024]{1,0:T(8,128)(2,1)} async-done(((bf16[1024,1024]{1,0:T(8,128)(2,1)}), bf16[128,1024]{1,0:T(8,128)(2,1)}) %reduce-scatter.49.cloned.1.call-update) | async-done | bytes 262160
  1316.8 69.6 %reduce-scatter.35.cloned.1.call-done = bf16[128,1024]{1,0:T(8,128)(2,1)} async-done(((bf16[1024,1024]{1,0:T(8,128)(2,1)}), bf16[128,1024]{1,0:T(8,128)(2,1)}) %reduce-scatter.35.cloned.1.call-update) | async-done | bytes 262160 | tf_op jit(solution)/shard_map/reduce_scatter | solution.py:276
  1386.5 70.9 %reduce-scatter.33.cloned.1.call-done = bf16[128,1024]{1,0:T(8,128)(2,1)} async-done(((bf16[1024,1024]{1,0:T(8,128)(2,1)}), bf16[128,1024]{1,0:T(8,128)(2,1)}) %reduce-scatter.33.cloned.1.call-update) | async-done | bytes 262160 | tf_op jit(solution)/shard_map/reduce_scatter | solution.py:276
  (427 shorter events, 122.6 us)
Async XLA Ops:
  7.2 71.9 %copy-start.83 = (u32[32]{0:T(128)S(1)}, u32[32]{0:T(128)}, u32[]{:S(2)}) copy-start(u32[32]{0:T(128)} %constant.123) | copy-start | bytes 388
  7.2 70.8 %copy-start.2 = (bf16[1024,1024]{1,0:T(8,128)(2,1)S(1)}, bf16[1024,1024]{1,0:T(8,128)(2,1)}, u32[]{:S(2)}) copy-start(bf16[1024,1024]{1,0:T(8,128)(2,1)} %param.12) | copy-start | bytes 6291460
  7.2 120.9 %all-gather.27.cloned.1.call-start = ((), (), s32[]{:S(2)}) async-start(), calls=%async_computation.17 | async-start | bytes 1769472 | tf_op jit(solution)/shard_map/all_gather | solution.py:89
  9.2 137.1 %all-gather.29.cloned.1.call-start = ((), (), s32[]{:S(2)}) async-start(), calls=%async_computation.18 | async-start | bytes 2359296 | tf_op jit(solution)/shard_map/all_gather | solution.py:93
  11.1 154.8 %all-gather.31.cloned.1.call-start = ((), (), s32[]{:S(2)}) async-start(), calls=%async_computation.19 | async-start | bytes 2359296 | tf_op jit(solution)/shard_map/all_gather | solution.py:95
  13.1 286.5 %all-reduce.16.cloned.1.call-start = ((), (), s32[]{:S(2)}) async-start(), calls=%async_computation.12 | async-start | bytes 4194304 | tf_op jit(solution)/shard_map/psum | solution.py:146
  59.1 72.8 %copy-start.76 = (f32[1,1,1024]{2,1,0:T(1,128)}, f32[1,1,1024]{2,1,0:T(1,128)S(1)}, u32[]{:S(2)}) copy-start(f32[1,1,1024]{2,1,0:T(1,128)S(1)} %get-tuple-element.101) | copy-start | bytes 12292
  78.0 53.9 %copy-start.62 = (f32[1,1,1024]{2,1,0:T(1,128)}, f32[1,1,1024]{2,1,0:T(1,128)S(1)}, u32[]{:S(2)}) copy-start(f32[1,1,1024]{2,1,0:T(1,128)S(1)} %get-tuple-element.99) | copy-start | bytes 12292
  78.4 53.5 %copy-start.48 = (f32[1024]{0:T(1024)}, f32[1024]{0:T(1024)S(1)}, u32[]{:S(2)}) copy-start(f32[1024]{0:T(1024)S(1)} %broadcast_multiply_fusion.10) | copy-start | bytes 12292
  79.1 52.8 %copy-start.60 = (f32[1024]{0:T(1024)}, f32[1024]{0:T(1024)S(1)}, u32[]{:S(2)}) copy-start(f32[1024]{0:T(1024)S(1)} %add_rsqrt_fusion.1) | copy-start | bytes 12292
  128.1 42.4 %copy-start.15 = (bf16[1,256,1024]{2,1,0:T(8,128)(2,1)}, bf16[1,256,1024]{2,1,0:T(8,128)(2,1)S(1)}, u32[]{:S(2)}) copy-start(bf16[1,256,1024]{2,1,0:T(8,128)(2,1)S(1)} %all-gather.4) | copy-start | bytes 1572868
  137.6 8.0 copy-start.34
  146.3 24.2 %copy-start.13 = (bf16[32,8,2,512]{3,1,2,0:T(8,128)(2,1)}, bf16[32,8,2,512]{3,1,2,0:T(8,128)(2,1)S(1)}, u32[]{:S(2)}) copy-start(bf16[32,8,2,512]{3,1,2,0:T(8,128)(2,1)S(1)} %copy.171) | copy-start | bytes 1572868
  172.6 130.8 %all-gather.33.cloned.1.call-start = ((), (), s32[]{:S(2)}) async-start(), calls=%async_computation.20 | async-start | bytes 1769472 | tf_op jit(solution)/shard_map/all_gather | solution.py:89
  173.2 172.8 %all-gather.35.cloned.1.call-start = ((), (), s32[]{:S(2)}) async-start(), calls=%async_computation.21 | async-start | bytes 2359296 | tf_op jit(solution)/shard_map/all_gather | solution.py:93
  173.8 196.0 %all-gather.37.cloned.1.call-start = ((), (), s32[]{:S(2)}) async-start(), calls=%async_computation.22 | async-start | bytes 2359296 | tf_op jit(solution)/shard_map/all_gather | solution.py:95
  174.5 291.6 %all-reduce.20.cloned.1.call-start = ((), (), s32[]{:S(2)}) async-start(), calls=%async_computation.32 | async-start | bytes 8388608 | tf_op jit(solution)/shard_map/psum | solution.py:252
  203.5 42.8 %copy-start.84 = (bf16[2,128]{1,0:T(2,128)(2,1)S(1)}, bf16[2,128]{1,0:T(2,128)(2,1)}, u32[]{:S(2)}) copy-start(bf16[2,128]{1,0:T(2,128)(2,1)} %param.23) | copy-start | bytes 1540
  203.5 59.8 %copy-start.85 = (bf16[2,128]{1,0:T(2,128)(2,1)S(1)}, bf16[2,128]{1,0:T(2,128)(2,1)}, u32[]{:S(2)}) copy-start(bf16[2,128]{1,0:T(2,128)(2,1)} %param.19) | copy-start | bytes 1540
  203.5 78.7 %copy-start.88 = (bf16[1,128]{1,0:T(2,128)(2,1)S(1)}, bf16[1,128]{1,0:T(2,128)(2,1)}, u32[]{:S(2)}) copy-start(bf16[1,128]{1,0:T(2,128)(2,1)} %get-tuple-element.113) | copy-start | bytes 772
  227.3 76.2 %copy-start.80 = (f32[1,1,1024]{2,1,0:T(1,128)}, f32[1,1,1024]{2,1,0:T(1,128)S(1)}, u32[]{:S(2)}) copy-start(f32[1,1,1024]{2,1,0:T(1,128)S(1)} %get-tuple-element.97) | copy-start | bytes 12292
  246.3 57.1 %copy-start.57 = (f32[1,1,1024]{2,1,0:T(1,128)}, f32[1,1,1024]{2,1,0:T(1,128)S(1)}, u32[]{:S(2)}) copy-start(f32[1,1,1024]{2,1,0:T(1,128)S(1)} %get-tuple-element.95) | copy-start | bytes 12292
  263.3 40.1 %copy-start.36 = (f32[1,1024]{1,0:T(1,128)}, f32[1,1024]{1,0:T(1,128)S(1)}, u32[]{:S(2)}) copy-start(f32[1,1024]{1,0:T(1,128)S(1)} %convert_element_type.324) | copy-start | bytes 12292
  282.2 21.3 %copy-start.40 = (f32[1,1024]{1,0:T(1,128)}, f32[1,1024]{1,0:T(1,128)S(1)}, u32[]{:S(2)}) copy-start(f32[1,1024]{1,0:T(1,128)S(1)} %convert_element_type.323) | copy-start | bytes 12292
  316.7 7.3 copy-start.1
  369.7 8.8 copy-start.93
  382.2 265.6 %all-reduce.18.cloned.1.call-start = ((), (), s32[]{:S(2)}) async-start(), calls=%async_computation.31 | async-start | bytes 12582912 | tf_op jit(solution)/shard_map/psum | solution.py:146
  383.3 7.0 copy-start.92
  383.3 7.0 copy-start.96
  392.6 73.5 %copy-start.38 = (f32[1,1024]{1,0:T(1,128)S(1)}, f32[1,1024]{1,0:T(1,128)}, u32[]{:S(2)}) copy-start(f32[1,1024]{1,0:T(1,128)} %copy-done.36) | copy-start | bytes 12292
  392.6 73.5 %copy-start.42 = (f32[1,1024]{1,0:T(1,128)S(1)}, f32[1,1024]{1,0:T(1,128)}, u32[]{:S(2)}) copy-start(f32[1,1024]{1,0:T(1,128)} %copy-done.40) | copy-start | bytes 12292
  392.7 73.5 %copy-start.46 = (f32[1024]{0:T(1024)S(1)}, f32[1024]{0:T(1024)}, u32[]{:S(2)}) copy-start(f32[1024]{0:T(1024)} %copy-done.44) | copy-start | bytes 12292
  392.7 73.4 %copy-start.52 = (f32[1024]{0:T(1024)S(1)}, f32[1024]{0:T(1024)}, u32[]{:S(2)}) copy-start(f32[1024]{0:T(1024)} %copy-done.50) | copy-start | bytes 12292
  392.7 73.4 %copy-start.55 = (f32[1,1,1024]{2,1,0:T(1,128)S(1)}, f32[1,1,1024]{2,1,0:T(1,128)}, u32[]{:S(2)}) copy-start(f32[1,1,1024]{2,1,0:T(1,128)} %get-tuple-element.96) | copy-start | bytes 12292
  392.7 73.4 %copy-start.58 = (f32[1,1,1024]{2,1,0:T(1,128)S(1)}, f32[1,1,1024]{2,1,0:T(1,128)}, u32[]{:S(2)}) copy-start(f32[1,1,1024]{2,1,0:T(1,128)} %copy-done.57) | copy-start | bytes 12292
  466.1 7.8 copy-start.4
  466.1 7.8 copy-start.5
  466.2 7.8 copy-start.6
  466.2 7.8 copy-start.21
  474.0 7.8 copy-start.16
  486.7 11.2 slice-start
  527.9 7.2 copy-start.69
  527.9 7.2 copy-start.68
  527.9 8.2 copy-start.14
  527.9 192.3 %reduce-scatter.47.cloned.1.call-start = ((), (), s32[]{:S(2)}) async-start(), calls=%async_computation.28 | async-start | bytes 589824
  534.1 245.4 %reduce-scatter.39.cloned.1.call-start = ((), (), s32[]{:S(2)}) async-start(), calls=%async_computation.24 | async-start | bytes 294912
  535.1 308.7 %reduce-scatter.43.cloned.1.call-start = ((), (), s32[]{:S(2)}) async-start(), calls=%async_computation.26 | async-start | bytes 294912
  536.1 373.3 %reduce-scatter.45.cloned.1.call-start = ((), (), s32[]{:S(2)}) async-start(), calls=%async_computation.27 | async-start | bytes 589824
  539.5 440.9 %reduce-scatter.51.cloned.1.call-start = ((), (), s32[]{:S(2)}) async-start(), calls=%async_computation.30 | async-start | bytes 2359296
  549.9 498.4 %reduce-scatter.31.cloned.1.call-start = ((), (), s32[]{:S(2)}) async-start(), calls=%async_computation.14 | async-start | bytes 1769472 | tf_op jit(solution)/shard_map/reduce_scatter | solution.py:264
  556.2 91.6 %copy-start.64 = (f32[1,1,1024]{2,1,0:T(1,128)S(1)}, f32[1,1,1024]{2,1,0:T(1,128)}, u32[]{:S(2)}) copy-start(f32[1,1,1024]{2,1,0:T(1,128)} %get-tuple-element.100) | copy-start | bytes 12292
  556.2 559.7 %reduce-scatter.29.cloned.1.call-start = ((), (), s32[]{:S(2)}) async-start(), calls=%async_computation.13 | async-start | bytes 1769472 | tf_op jit(solution)/shard_map/reduce_scatter | solution.py:264
  561.2 619.4 %reduce-scatter.37.cloned.1.call-start = ((), (), s32[]{:S(2)}) async-start(), calls=%async_computation.23 | async-start | bytes 294912
  658.4 586.4 %reduce-scatter.41.cloned.1.call-start = ((), (), s32[]{:S(2)}) async-start(), calls=%async_computation.25 | async-start | bytes 294912
  659.4 656.3 %reduce-scatter.49.cloned.1.call-start = ((), (), s32[]{:S(2)}) async-start(), calls=%async_computation.29 | async-start | bytes 2359296
  669.6 6.8 copy-start.75
  669.6 716.8 %reduce-scatter.35.cloned.1.call-start = ((), (), s32[]{:S(2)}) async-start(), calls=%async_computation.16 | async-start | bytes 2359296 | tf_op jit(solution)/shard_map/reduce_scatter | solution.py:276
  676.3 26.2 %copy-start.87 = (bf16[1,128]{1,0:T(2,128)(2,1)S(1)}, bf16[1,128]{1,0:T(2,128)(2,1)}, u32[]{:S(2)}) copy-start(bf16[1,128]{1,0:T(2,128)(2,1)} %get-tuple-element.109) | copy-start | bytes 772
  676.3 43.8 %copy-start.65 = (bf16[4,3,64]{2,0,1:T(4,128)(2,1)S(1)}, bf16[4,3,64]{2,0,1:T(4,128)(2,1)}, u32[]{:S(2)}) copy-start(bf16[4,3,64]{2,0,1:T(4,128)(2,1)} %get-tuple-element.46) | copy-start | bytes 4612
  676.4 45.0 %copy-start.70 = (bf16[1024]{0:T(1024)(128)(2,1)S(1)}, bf16[1024]{0:T(1024)(128)(2,1)}, u32[]{:S(2)}) copy-start(bf16[1024]{0:T(1024)(128)(2,1)} %get-tuple-element.41) | copy-start | bytes 6148
  676.4 44.9 %copy-start.71 = (bf16[1024]{0:T(1024)(128)(2,1)S(1)}, bf16[1024]{0:T(1024)(128)(2,1)}, u32[]{:S(2)}) copy-start(bf16[1024]{0:T(1024)(128)(2,1)} %get-tuple-element.52) | copy-start | bytes 6148
  676.4 44.9 %copy-start.89 = (bf16[1024]{0:T(1024)(128)(2,1)S(1)}, bf16[1024]{0:T(1024)(128)(2,1)}, u32[]{:S(2)}) copy-start(bf16[1024]{0:T(1024)(128)(2,1)} %get-tuple-element.129) | copy-start | bytes 6148
  676.4 781.0 %reduce-scatter.33.cloned.1.call-start = ((), (), s32[]{:S(2)}) async-start(), calls=%async_computation.15 | async-start | bytes 2359296 | tf_op jit(solution)/shard_map/reduce_scatter | solution.py:276
  756.4 704.1 %copy-start.74 = (f32[2,128]{1,0:T(2,128)}, f32[2,128]{1,0:T(2,128)S(1)}, u32[]{:S(2)}) copy-start(f32[2,128]{1,0:T(2,128)S(1)} %maximum_convert_fusion.9) | copy-start | bytes 3076
  (59 other events, 216.2 us)
Sparse Core Ops, SparseCore 0:
  10.8 47.0 all-gather.26
  60.5 50.5 all-gather.28
  113.7 52.1 all-gather.30
  172.7 49.5 all-reduce.15
  224.9 44.3 all-gather.32
  271.4 47.4 all-gather.34
  320.9 48.8 all-gather.36
  382.4 83.6 all-reduce.19
  528.0 119.7 all-reduce.17
  651.6 62.8 reduce-scatter.46
  718.4 61.0 reduce-scatter.38
  782.7 61.1 reduce-scatter.42
  847.7 61.6 reduce-scatter.44
  912.8 67.4 reduce-scatter.50
  983.6 64.5 reduce-scatter.30
  1051.5 64.3 reduce-scatter.28
  1119.7 60.8 reduce-scatter.36
  1183.7 61.0 reduce-scatter.40
  1248.4 67.2 reduce-scatter.48
  1319.1 67.3 reduce-scatter.34
  1390.0 67.2 reduce-scatter.32
where the time goes:
time: 1470 us
  waiting for transfers between devices  855 us (58%)
  blocking collectives  290 us (20%)
  matrix products  156 us (11%)
  local copies, waits for them, and re-layouts  79.7 us (5%)
  other arithmetic  68 us (5%)
  between operations  18.5 us (1%)
    unnamed x29, waiting for transfers between devices  408 us
    reduce_scatter x2, waiting for transfers between devices, per_device(): lax.psum_scatter(d_up.astype(jnp.bfloat16), 'shard', scatter_dimension=0,...  141 us
    reduce_scatter x2, waiting for transfers between devices, per_device(): lax.psum_scatter(d_qkv.astype(jnp.bfloat16), 'shard', scatter_dimension=0...  134 us
    psum x2, waiting for transfers between devices, per_device(): lax.psum(partial_branch.astype(jnp.bfloat16), 'tensor').astype(jnp.float32)  86.6 us
    psum x1, waiting for transfers between devices, per_device(): lax.psum(d_first.astype(jnp.bfloat16), 'tensor').astype(jnp.float32)  71.3 us
    all_gather x2, blocking collectives, per_device(): lax.all_gather(w_dense[layer], 'shard', axis=1, tiled=True)  56.9 us
    unnamed x2, blocking collectives  53.1 us
    all_gather x2, blocking collectives, per_device(): lax.all_gather(b_fc1[layer], 'shard', axis=0, tiled=True)  39 us
  transfers between devices with their start and end apart: 21, of which 15 were waited for; matrix products, arithmetic and copies ran while one was open for 14% of the time, Pallas kernels for 0%

commit v1 on v0

v1 whole, which is shorter than its diff:
```python
import math

import jax
import jax.numpy as jnp
from jax import lax
from jax.sharding import PartitionSpec as P

HD = 64
ROT = 16
LAYERS = 2
LEN = 512
BF = jnp.bfloat16
F32 = jnp.float32


def ring_order(count):
    return list(range(0, count, 2)) + list(range(count - 1, 0, -2))


def ring_perms(count):
    order = ring_order(count)
    ahead = [(order[i], order[(i + 1) % count]) for i in range(count)]
    return ahead, [(b, a) for a, b in ahead]


def after(value, *others):
    return lax.optimization_barrier((value,) + others)[0]


class Ring:
    def __init__(self):
        self.count = lax.axis_size("shard")
        self.order = ring_order(self.count)
        self.ahead, self.back = ring_perms(self.count)
        table = [0] * self.count
        for place, device in enumerate(self.order):
            table[device] = place
        me = lax.axis_index("shard")
        place = jnp.array(table, jnp.int32)[me]
        owners = jnp.array(self.order, jnp.int32)
        self.owner = [owners[(place + step) % self.count] for step in range(self.count)]
        self.me = me

    def gather(self, part, gate=None):
        count, half = self.count, part.shape[1] // 2
        whole = jnp.zeros((count,) + part.shape, part.dtype)

        def put(whole, piece, owner, col=0):
            return lax.dynamic_update_slice(whole, piece[None], (owner, 0, col))

        whole = put(whole, part, self.me)
        if gate is not None:
            part = after(part, gate)
        up = down = part
        for step in range(1, count // 2):
            up = lax.ppermute(up, "shard", self.ahead)
            down = lax.ppermute(down, "shard", self.back)
            whole = put(whole, up, self.owner[count - step])
            whole = put(whole, down, self.owner[step])
        gate = (up, down)
        left = lax.ppermute(up[:, :half], "shard", self.ahead)
        right = lax.ppermute(down[:, half:], "shard", self.back)
        far = count // 2
        whole = put(whole, left, self.owner[far])
        whole = put(whole, right, self.owner[far], half)
        return whole.reshape(count * part.shape[0], part.shape[1]), gate

    def scatter(self, total, gate=None):
        count = self.count
        rows, cols = total.shape[0] // count, total.shape[1]
        half = cols // 2

        def piece(step, lo=0, hi=None):
            hi = cols if hi is None else hi
            return lax.dynamic_slice(total, (self.owner[step % count] * rows, lo), (rows, hi - lo))

        far = count // 2
        head_up, head_down = piece(far, 0, half), piece(far, half, cols)
        if gate is not None:
            head_up, head_down = after(head_up, gate), after(head_down, gate)
        head_up = lax.ppermute(head_up, "shard", self.ahead)
        head_down = lax.ppermute(head_down, "shard", self.back)
        up = jnp.concatenate(
            [
                (piece(far - 1, 0, half).astype(F32) + head_up.astype(F32)).astype(BF),
                piece(far - 1, half, cols),
            ],
            axis=1,
        )
        down = jnp.concatenate(
            [
                piece(far + 1, 0, half),
                (piece(far + 1, half, cols).astype(F32) + head_down.astype(F32)).astype(BF),
            ],
            axis=1,
        )
        for step in range(far - 1, 0, -1):
            up = lax.ppermute(up, "shard", self.ahead)
            down = lax.ppermute(down, "shard", self.back)
            if step > 1:
                up = (up.astype(F32) + piece(step - 1).astype(F32)).astype(BF)
                down = (down.astype(F32) + piece(count - step + 1).astype(F32)).astype(BF)
        return up.astype(F32) + down.astype(F32) + piece(0).astype(F32), (up, down)

    def small_sum(self, value):
        total = value
        for step in range(1, self.count):
            perm = [(i, (i + step) % self.count) for i in range(self.count)]
            total = total + lax.ppermute(value, "shard", perm)
        return total


def partner(bit):
    count = lax.axis_size("tensor")
    return [(i, i ^ (1 << bit)) for i in range(count)]


def tensor_bits():
    return lax.axis_size("tensor").bit_length() - 1


def tensor_scatter(part):
    me = lax.axis_index("tensor")
    for bit in range(tensor_bits()):
        rows = part.shape[0] // 2
        side = (me >> bit) & 1
        keep = lax.dynamic_slice_in_dim(part, side * rows, rows, 0)
        give = lax.dynamic_slice_in_dim(part, (1 - side) * rows, rows, 0)
        got = lax.ppermute(give.astype(BF), "tensor", partner(bit))
        part = keep.astype(F32) + got.astype(F32)
    return part


def tensor_own(part):
    me = lax.axis_index("tensor")
    for bit in range(tensor_bits()):
        rows = part.shape[0] // 2
        part = lax.dynamic_slice_in_dim(part, ((me >> bit) & 1) * rows, rows, 0)
    return part


def tensor_gather(part):
    me = lax.axis_index("tensor")
    for bit in reversed(range(tensor_bits())):
        got = lax.ppermute(part, "tensor", partner(bit))
        side = (me >> bit) & 1
        part = jnp.where(
            side == 0, jnp.concatenate([part, got], axis=0), jnp.concatenate([got, part], axis=0)
        )
    return part


def tensor_small_sum(value):
    for bit in range(tensor_bits()):
        value = value + lax.ppermute(value, "tensor", partner(bit))
    return value


def rotate_tables():
    half = ROT // 2
    places = jnp.arange(LEN).astype(F32)
    freqs = jnp.exp(-(2.0 * jnp.arange(half).astype(F32) / ROT) * math.log(10000.0))
    angles = places[:, None] * freqs[None, :]
    angles = jnp.concatenate([angles, angles], axis=1)
    return (jnp.cos(angles)[:, None, :], jnp.sin(angles)[:, None, :])


def rotate(part, cosine, sine):
    inner = part[..., :ROT]
    lower = inner[..., : ROT // 2]
    upper = inner[..., ROT // 2 :]
    turned = inner * cosine + jnp.concatenate([-upper, lower], axis=-1) * sine
    return jnp.concatenate([turned, part[..., ROT:]], axis=-1)


def rotate_back(grad, cosine, sine):
    inner = grad[..., :ROT]
    scaled = inner * sine
    lower = scaled[..., : ROT // 2]
    upper = scaled[..., ROT // 2 :]
    turned = inner * cosine + jnp.concatenate([upper, -lower], axis=-1)
    return jnp.concatenate([turned, grad[..., ROT:]], axis=-1)


def attend(joined, tables):
    heads = joined.shape[1] // (3 * HD)
    joined = joined.reshape(LEN, 3, heads, HD)
    queries = rotate(joined[:, 0], *tables).astype(BF)
    key_rows = rotate(joined[:, 1], *tables).astype(BF)
    value_rows = joined[:, 2].astype(BF)
    scores = jnp.einsum("qhd,khd->hqk", queries, key_rows, preferred_element_type=F32)
    scores = scores * (1.0 / math.sqrt(HD))
    causal = jnp.arange(LEN)[:, None] >= jnp.arange(LEN)[None, :]
    scores = jnp.where(causal, scores, -1e30)
    highest = jnp.max(scores, axis=-1, keepdims=True)
    log_total = highest + jnp.log(jnp.sum(jnp.exp(scores - highest), axis=-1, keepdims=True))
    chances = jnp.exp(scores - log_total).astype(BF)
    mixed = jnp.einsum("hqk,khd->qhd", chances, value_rows, preferred_element_type=F32)
    return mixed.astype(BF).reshape(LEN, heads * HD), (queries, key_rows, value_rows, log_total)


def attend_back(d_mixed, kept, tables):
    queries, key_rows, value_rows, log_total = kept
    heads = queries.shape[1]
    scores = jnp.einsum("qhd,khd->hqk", queries, key_rows, preferred_element_type=F32)
    scores = scores * (1.0 / math.sqrt(HD))
    causal = jnp.arange(LEN)[:, None] >= jnp.arange(LEN)[None, :]
    chances = jnp.exp(jnp.where(causal, scores, -1e30) - log_total)
    d_mixed = d_mixed.reshape(LEN, heads, HD)
    d_value = jnp.einsum("hqk,qhd->khd", chances.astype(BF), d_mixed, preferred_element_type=F32)
    d_chances = jnp.einsum("qhd,khd->hqk", d_mixed, value_rows, preferred_element_type=F32)
    row_inner = jnp.sum(chances * d_chances, axis=-1, keepdims=True)
    d_scores = (chances * (d_chances - row_inner)).astype(BF)
    scale = 1.0 / math.sqrt(HD)
    d_query = jnp.einsum("hqk,khd->qhd", d_scores, key_rows, preferred_element_type=F32) * scale
    d_key = jnp.einsum("hqk,qhd->khd", d_scores, queries, preferred_element_type=F32) * scale
    d_joined = jnp.stack(
        [rotate_back(d_query, *tables), rotate_back(d_key, *tables), d_value], axis=1
    )
    return d_joined.astype(BF).reshape(LEN, 3 * heads * HD)


def normalize(resid):
    centered = resid - jnp.mean(resid, axis=-1, keepdims=True)
    factor = lax.rsqrt(jnp.mean(centered * centered, axis=-1, keepdims=True) + 1e-05)
    return (centered * factor, factor)


def gelu_both(hidden_in):
    normal_cdf = 0.5 * (1.0 + jax.scipy.special.erf(hidden_in * (1.0 / math.sqrt(2.0))))
    density = jnp.exp(-0.5 * hidden_in * hidden_in) * (1.0 / math.sqrt(2.0 * math.pi))
    return hidden_in * normal_cdf, normal_cdf + hidden_in * density


def by_kind(mat):
    lead, cols = mat.shape[:-1], mat.shape[-1]
    mat = mat.reshape(lead + (cols // (3 * HD), 3, HD))
    return jnp.swapaxes(mat, -3, -2).reshape(lead + (cols,))


def by_head(mat):
    lead, cols = mat.shape[:-1], mat.shape[-1]
    mat = mat.reshape(lead + (3, cols // (3 * HD), HD))
    return jnp.swapaxes(mat, -3, -2).reshape(lead + (cols,))


def per_device(
    tokens, cotangent, ln_gain, ln_bias, w_qkv, b_qkv, w_dense, b_dense, w_fc1, b_fc1, w_fc2, b_fc2
):
    streams = tokens.shape[0] // LEN
    model = tokens.shape[1]
    qkv_cols, ff_cols = w_qkv.shape[2], w_fc1.shape[2]
    mix_cols = qkv_cols // 3
    in_cols = qkv_cols + ff_cols
    ring = Ring()
    count, me = ring.count, ring.me
    tables = rotate_tables()
    gains, shifts = ln_gain.astype(F32), ln_bias.astype(F32)

    raw_in, parts_qkv, parts_up, parts_out, smalls = [], [], [], [], []
    for layer in range(LAYERS):
        raw = jnp.concatenate([by_kind(w_qkv[layer]), w_fc1[layer]], axis=1).astype(F32)
        raw_in.append(raw)
        gain = jnp.concatenate(
            [
                jnp.broadcast_to(gains[layer, k][:, None], (raw.shape[0], width))
                for k, width in ((0, qkv_cols), (1, ff_cols))
            ],
            axis=1,
        )
        scaled = (raw * gain).astype(BF)
        parts_qkv.append(scaled[:, :qkv_cols])
        parts_up.append(scaled[:, qkv_cols:])
        parts_out.append(
            jnp.concatenate([w_dense[layer].T, w_fc2[layer].T], axis=1)
        )
        moved = jnp.concatenate(
            [
                jnp.sum(raw[:, :qkv_cols] * shifts[layer, 0][:, None], axis=0),
                jnp.sum(raw[:, qkv_cols:] * shifts[layer, 1][:, None], axis=0),
            ]
        )
        own = jnp.zeros((qkv_cols,), F32)
        own = lax.dynamic_update_slice(
            own, b_qkv[layer].astype(F32), (me * b_qkv.shape[1],)
        )
        own_up = lax.dynamic_update_slice(
            jnp.zeros((ff_cols,), F32), b_fc1[layer].astype(F32), (me * b_fc1.shape[1],)
        )
        own_out = lax.dynamic_update_slice(
            jnp.zeros((model,), F32),
            b_dense[layer].astype(F32) + b_fc2[layer].astype(F32),
            (me * b_dense.shape[1],),
        )
        smalls.append(
            jnp.concatenate([moved + jnp.concatenate([by_kind(own), own_up]), own_out])
        )
    biases = ring.small_sum(jnp.stack(smalls))

    gate = None
    mats = []
    for layer in range(LAYERS):
        qkv_mat, gate = ring.gather(parts_qkv[layer], gate)
        up_mat, gate = ring.gather(parts_up[layer], gate)
        out_mat, gate = ring.gather(parts_out[layer], gate)
        mats.append((qkv_mat, up_mat, out_mat))

    token_streams = [tokens[i * LEN : (i + 1) * LEN].astype(F32) for i in range(streams)]
    resid = [tensor_own(item) for item in token_streams]
    stored = [[None] * streams for _ in range(LAYERS)]
    outputs = []
    for layer in range(LAYERS):
        qkv_mat, up_mat, out_mat = mats[layer]
        for i in range(streams):
            own_normed, factor = normalize(resid[i])
            if layer == 0:
                normed = normalize(token_streams[i])[0].astype(BF)
            else:
                normed = tensor_gather(own_normed.astype(BF))
            joined = (
                jnp.dot(normed, qkv_mat, preferred_element_type=F32) + biases[layer, :qkv_cols]
            )
            mixed, kept = attend(joined, tables)
            hidden_in = (
                jnp.dot(normed, up_mat, preferred_element_type=F32)
                + biases[layer, qkv_cols:in_cols]
            )
            hidden, slope = gelu_both(hidden_in)
            hidden, slope = hidden.astype(BF), slope.astype(BF)
            both = jnp.concatenate([mixed, hidden], axis=1)
            partial = lax.dot_general(
                both, out_mat, (((1,), (1,)), ((), ())), preferred_element_type=F32
            ).astype(BF)
            branch = tensor_scatter(partial) + biases[layer, in_cols:]
            stored[layer][i] = (normed, own_normed, factor, kept, slope, both)
            resid[i] = resid[i] + branch
    for i in range(streams):
        outputs.append(tensor_gather(resid[i].astype(BF)))

    cotangent_streams = [cotangent[i * LEN : (i + 1) * LEN] for i in range(streams)]
    grad = [tensor_own(item).astype(F32) for item in cotangent_streams]
    grad_low = cotangent_streams
    gate = None
    in_grads, out_grads, small_grads = [None] * LAYERS, [None] * LAYERS, [None] * LAYERS
    for layer in reversed(range(LAYERS)):
        qkv_mat, up_mat, out_mat = mats[layer]
        low = jnp.concatenate(grad_low, axis=0)
        both = jnp.concatenate([item[5] for item in stored[layer]], axis=0)
        d_out = lax.dot_general(
            low, both, (((0,), (0,)), ((), ())), preferred_element_type=F32
        ).astype(BF)
        out_grads[layer], gate = ring.scatter(d_out, gate)
        d_ins = []
        for i in range(streams):
            normed, own_normed, factor, kept, slope, _ = stored[layer][i]
            d_both = jnp.dot(grad_low[i], out_mat, preferred_element_type=F32)
            d_mixed = d_both[:, :mix_cols].astype(BF)
            d_hidden_in = (d_both[:, mix_cols:] * slope.astype(F32)).astype(BF)
            d_joined = attend_back(d_mixed, kept, tables)
            d_in = jnp.concatenate([d_joined, d_hidden_in], axis=1)
            d_ins.append(d_in)
            in_mat = jnp.concatenate([qkv_mat, up_mat], axis=1)
            shaped = lax.dot_general(
                d_in, in_mat, (((1,), (1,)), ((), ())), preferred_element_type=F32
            ).astype(BF)
            shaped = tensor_scatter(shaped)
            grad[i] = grad[i] + factor * (
                shaped
                - jnp.mean(shaped, axis=-1, keepdims=True)
                - own_normed * jnp.mean(shaped * own_normed, axis=-1, keepdims=True)
            )
        d_in = jnp.concatenate(d_ins, axis=0)
        normed = jnp.concatenate([item[0] for item in stored[layer]], axis=0)
        d_in_mat = lax.dot_general(
            normed, d_in, (((0,), (0,)), ((), ())), preferred_element_type=F32
        ).astype(BF)
        in_grads[layer], gate = ring.scatter(d_in_mat, gate)
        small_grads[layer] = jnp.concatenate(
            [jnp.sum(d_in.astype(F32), axis=0), jnp.sum(low.astype(F32), axis=0)]
        )
        grad_low = [tensor_gather(item.astype(BF)) for item in grad]

    d_tokens = jnp.concatenate(grad_low, axis=0)
    output = jnp.concatenate(outputs, axis=0)
    sums = [ring.small_sum(item) for item in small_grads]

    results = []
    norm_sums = []
    for layer in range(LAYERS):
        grads, sum_in, raw = in_grads[layer], sums[layer][:in_cols], raw_in[layer]
        weighted, moved = raw * grads, raw * sum_in[None, :]
        norm_sums.append(
            jnp.stack(
                [
                    jnp.sum(weighted[:, :qkv_cols], axis=1),
                    jnp.sum(weighted[:, qkv_cols:], axis=1),
                    jnp.sum(moved[:, :qkv_cols], axis=1),
                    jnp.sum(moved[:, qkv_cols:], axis=1),
                ]
            )
        )
        d_qkv = (
            gains[layer, 0][:, None] * grads[:, :qkv_cols]
            + shifts[layer, 0][:, None] * sum_in[None, :qkv_cols]
        )
        d_up = (
            gains[layer, 1][:, None] * grads[:, qkv_cols:]
            + shifts[layer, 1][:, None] * sum_in[None, qkv_cols:]
        )
        d_qkv_bias = by_head(sum_in[:qkv_cols])
        results.append(
            (
                by_head(d_qkv),
                lax.dynamic_slice(d_qkv_bias, (me * b_qkv.shape[1],), (b_qkv.shape[1],)),
                out_grads[layer][:, :mix_cols].T,
                lax.dynamic_slice(
                    sums[layer], (in_cols + me * b_dense.shape[1],), (b_dense.shape[1],)
                ),
                d_up,
                lax.dynamic_slice(
                    sums[layer], (qkv_cols + me * b_fc1.shape[1],), (b_fc1.shape[1],)
                ),
                out_grads[layer][:, mix_cols:].T,
            )
        )
    norm_sums = tensor_small_sum(jnp.stack(norm_sums))

    def stacked(index):
        return jnp.stack([results[layer][index] for layer in range(LAYERS)])

    return (
        output,
        d_tokens,
        norm_sums[:, :2],
        norm_sums[:, 2:],
        stacked(0),
        stacked(1),
        stacked(2),
        stacked(3),
        stacked(4),
        stacked(5),
        stacked(6),
        stacked(3),
    )


def solution(mesh):
    in_specs = (
        P("shard", None),
        P("shard", None),
        P(None, None, "shard"),
        P(None, None, "shard"),
        P(None, "shard", "tensor"),
        P(None, ("tensor", "shard")),
        P(None, "tensor", "shard"),
        P(None, "shard"),
        P(None, "shard", "tensor"),
        P(None, ("tensor", "shard")),
        P(None, "tensor", "shard"),
        P(None, "shard"),
    )
    out_specs = (
        P("shard", None),
        P("shard", None),
        P(None, None, "shard"),
        P(None, None, "shard"),
        P(None, "shard", "tensor"),
        P(None, ("tensor", "shard")),
        P(None, "tensor", "shard"),
        P(None, "shard"),
        P(None, "shard", "tensor"),
        P(None, ("tensor", "shard")),
        P(None, "tensor", "shard"),
        P(None, "shard"),
    )
    return jax.shard_map(
        per_device, mesh=mesh, in_specs=in_specs, out_specs=out_specs, check_vma=False
    )
```

time: 1470 us -> 777 us (0.53)
  waiting for transfers between devices: 855 us -> 185 us
  blocking collectives: 290 us -> 0 us
  starting transfers between devices: 1.33 us -> 140 us
  other arithmetic: 68 us -> 126 us
  local copies, waits for them, and re-layouts: 79.7 us -> 131 us
    unnamed x29 -> x0, waiting for transfers between devices: 408 us -> none
    reduce_scatter x4 -> x0, waiting for transfers between devices: 275 us -> none  [the longest x2 141 us: per_device(): lax.psum_scatter(d_up.astype(jnp.bfloat16), 'shard', scatter_dimension=0,...]
    all_gather x12 -> x0, blocking collectives: 237 us -> none  [the longest x2 56.9 us: per_device(): lax.all_gather(w_dense[layer], 'shard', axis=1, tiled=True)]
    ppermute x0 -> x135, waiting for transfers between devices: none -> 185 us  [the longest x18 32 us: gather(): up = lax.ppermute(up, 'shard', self.ahead)]
    psum x3 -> x0, waiting for transfers between devices: 158 us -> none  [the longest x2 86.6 us: per_device(): lax.psum(partial_branch.astype(jnp.bfloat16), 'tensor').astype(jnp.float32)]
    ppermute x0 -> x135, starting transfers between devices: none -> 140 us  [the longest x21 33.9 us: small_sum(): total = total + lax.ppermute(value, 'shard', perm)]
    unnamed x2 -> x0, blocking collectives: 53.1 us -> none
    dynamic_update_slice x0 -> x52, local copies, waits for them, and re-layouts: none -> 42.1 us  [put(): return lax.dynamic_update_slice(whole, piece[None], (owner, 0, col))]
  transfers between devices with their start and end apart: 21 -> 135, of which waited for: 15 -> 63; matrix products, arithmetic and copies ran while one was open for 14% -> 32% of each run, Pallas kernels for 0% -> 0%
where the time goes in v1:
time: 777 us; the launch traced here: 767 us
  waiting for transfers between devices  185 us (24%)
  matrix products  156 us (20%)
  starting transfers between devices  140 us (18%)
  local copies, waits for them, and re-layouts  131 us (17%)
  other arithmetic  126 us (16%)
  between operations  29.9 us (4%)
    dynamic_update_slice x52, local copies, waits for them, and re-layouts, put(): return lax.dynamic_update_slice(whole, piece[None], (owner, 0, col))  42.1 us
    ppermute x21, starting transfers between devices, small_sum(): total = total + lax.ppermute(value, 'shard', perm)  33.9 us
    ppermute x18, waiting for transfers between devices, gather(): up = lax.ppermute(up, 'shard', self.ahead)  32 us
    ppermute x16, waiting for transfers between devices, tensor_scatter(): got = lax.ppermute(give.astype(BF), 'tensor', partner(bit))  29 us
    ppermute x12, waiting for transfers between devices, scatter(): up = lax.ppermute(up, 'shard', self.ahead)  28.7 us
    reduce_sum x2, other arithmetic, per_device(): jnp.sum(d_in.astype(F32), axis=0)  26.1 us
    ppermute x12, waiting for transfers between devices, scatter(): down = lax.ppermute(down, 'shard', self.back)  23.3 us
    ppermute x18, starting transfers between devices, gather(): up = lax.ppermute(up, 'shard', self.ahead)  21.3 us
  transfers between devices with their start and end apart: 135, of which 63 were waited for; matrix products, arithmetic and copies ran while one was open for 32% of the time, Pallas kernels for 0%

profile of v1, /device:TPU:0, one launch (start us, length us, event | category | flops | bytes accessed | tf_op | source)
XLA Modules:
  0.0 767.1 jit_solution(12939208310922492667)
XLA Ops:
  5.2 4.0 collective-permute-start.10
  78.6 3.7 collective-permute-done.2
  86.1 3.2 collective-permute-done.4
  89.3 2.9 collective-permute-done.5
  106.9 3.5 convolution_add_fusion.1
  131.5 4.2 collective-permute-done.19
  142.8 4.1 collective-permute-done.21
  149.1 4.3 multiply_convert_fusion.8
  157.0 4.0 collective-permute-done.25
  168.1 3.0 collective-permute-done.28
  180.2 3.3 convolution_convert_fusion.7
  187.1 3.8 collective-permute-done.37
  194.4 3.0 collective-permute-done.39
  230.3 5.1 collective-permute-done.49
  243.8 3.6 convolution_add_fusion.2
  263.1 3.2 collective-permute-done.55
  276.0 3.3 convolution_bitcast_fusion.1
  283.2 4.0 multiply_reduce_fusion.3
  295.2 4.7 multiply_convert_fusion.7
  299.9 4.9 fusion.68
  304.9 3.3 convolution_convert_fusion.6
  312.6 6.9 collective-permute-done.72
  319.7 4.4 collective-permute-done.60
  327.1 5.8 collective-permute-done.73
  337.5 3.6 fusion.230
  341.4 8.7 %multiply_reduce_fusion.2 = (f32[4,512]{1,0:T(4,128)}, f32[4,512]{1,0:T(4,128)S(1)}, f32[4,512,512]{1,2,0:T(8,128)}) fusion(f32[4,512,512]{1,2,0:T(8,128)} %copy-done.4, f32[4,512]{1,0:T(4,128)S(1)} %log_add_fusion.3, pred[512,512]{0,1:T(8,128)(4,1)S(1)} %iota_compare_fusion, f32[4,512,512]{1,2,0:T(8,128)} %fusion.129, ...), kind=kOutput, calls=%fused_computation.9 | convolution fusion | flops 142602240 | bytes 13393920 | tf_op jit(solution)/shard_map/qhd,khd->hqk/dot_general | solution.py:211
  351.0 3.1 convolution_convert_fusion.13
  355.9 5.4 fusion.48
  361.3 3.7 convolution_convert_fusion.5
  378.2 5.3 collective-permute-done.61
  383.7 4.5 collective-permute-done.64
  391.5 3.3 convolution_bitcast_fusion
  403.0 4.1 fusion.101
  409.1 3.5 convolution_add_fusion
  412.6 3.0 copy.150
  417.2 5.5 fusion.47
  439.7 4.8 convolution_convert_fusion.4
  444.6 4.8 convolution_convert_fusion
  453.7 4.8 fusion.71
  458.6 16.0 %convolution_convert_fusion.2 = bf16[1024,1792]{1,0:T(8,128)(2,1)} fusion(bf16[512,1024]{1,0:T(8,128)(2,1)S(1)} %copy-done.70, bf16[512,1024]{1,0:T(8,128)(2,1)S(1)} %copy-done.67, bf16[512,1024]{1,0:T(8,128)(2,1)S(1)} %copy-done.65, bf16[512,768]{1,0:T(8,128)(2,1)S(1)} %copy-done.40, bf16[512,1024]{1,0:T(8,128)(2,1)S(1)} %copy-done.64, ...), kind=kOutput, calls=%fused_computation.26 | convolution fusion | flops 3778805760 | bytes 9437184 | tf_op jit(solution)/shard_map/dot_general | solution.py:374
  475.7 13.2 %convert_reduce_fusion = f32[1792]{0:T(1024)S(1)} fusion(bf16[512,1024]{1,0:T(8,128)(2,1)S(1)} %copy-done.65, bf16[512,768]{1,0:T(8,128)(2,1)S(1)} %copy-done.40, bf16[512,1024]{1,0:T(8,128)(2,1)S(1)} %copy-done.64, bf16[512,768]{1,0:T(8,128)(2,1)S(1)} %copy-done.37), kind=kLoop, calls=%fused_computation | loop fusion | flops 16513280 | bytes 3677184 | tf_op jit(solution)/shard_map/reduce_sum | solution.py:379
  496.1 3.0 collective-permute-start.87
  502.4 4.7 fusion.74
  540.5 10.6 %collective-permute-done.80 = bf16[128,1024]{1,0:T(8,128)(2,1)S(1)} collective-permute-done((bf16[128,1024]{1,0:T(8,128)(2,1)S(1)}, bf16[128,1024]{1,0:T(8,128)(2,1)S(1)}, u32[]{:S(2)}, u32[]{:S(2)}) %collective-permute-start.80) | collective-permute-done | bytes 262176 | tf_op jit(solution)/shard_map/ppermute | solution.py:129
  562.9 5.4 collective-permute-done.77
  577.0 3.3 collective-permute-done.99
  585.8 3.6 fusion.231
  591.1 4.0 multiply_reduce_fusion
  603.6 3.0 fusion.46
  606.7 12.8 %convert_reduce_fusion.1 = f32[1792]{0:T(1024)S(1)} fusion(bf16[512,1024]{1,0:T(8,128)(2,1)S(1)} %fusion.46, bf16[512,768]{1,0:T(8,128)(2,1)S(1)} %copy-done.39, bf16[512,1024]{1,0:T(8,128)(2,1)S(1)} %copy-done.62, bf16[512,768]{1,0:T(8,128)(2,1)S(1)} %copy-done.38), kind=kLoop, calls=%fused_computation.1 | loop fusion | flops 16513280 | bytes 3677184 | tf_op jit(solution)/shard_map/reduce_sum | solution.py:379
  619.6 4.2 convolution_convert_fusion.3
  624.5 4.0 fusion.77
  630.4 3.1 maximum_select_fusion.5
  644.2 3.1 convolution_convert_fusion.1
  647.3 5.2 collective-permute-done.101
  663.6 5.9 collective-permute-done.124
  681.4 4.3 collective-permute-done.104
  692.5 3.1 collective-permute-done.105
  702.4 3.3 collective-permute-done.106
  705.7 4.3 collective-permute-done.110
  713.6 5.0 collective-permute-done.115
  723.3 6.5 collective-permute-done.116
  735.5 9.4 %collective-permute-done.113 = bf16[128,1792]{1,0:T(8,128)(2,1)S(1)} collective-permute-done((bf16[128,1792]{1,0:T(8,128)(2,1)S(1)}, bf16[128,1792]{1,0:T(8,128)(2,1)S(1)}, u32[]{:S(2)}, u32[]{:S(2)}) %collective-permute-start.113) | collective-permute-done | bytes 458784 | tf_op jit(solution)/shard_map/ppermute | solution.py:98
  753.1 4.5 collective-permute-done.114
  (1102 shorter events, 427.4 us)
Async XLA Ops:
  5.2 37.5 %collective-permute-start.10 = (f32[2,2816]{1,0:T(2,128)}, f32[2,2816]{1,0:T(2,128)}, u32[]{:S(2)}, u32[]{:S(2)}) collective-permute-start(f32[2,2816]{1,0:T(2,128)} %pad_maximum_fusion.63), channel_id=1, source_target_pairs={{0,12},{4,16},{8,20},{12,24},{16,28},{20,0},{24,4},{28,8},{1,13},{... | collective-permute-start | bytes 67592 | tf_op jit(solution)/shard_map/ppermute | solution.py:109
  9.2 34.2 %collective-permute-start.11 = (f32[2,2816]{1,0:T(2,128)}, f32[2,2816]{1,0:T(2,128)}, u32[]{:S(2)}, u32[]{:S(2)}) collective-permute-start(f32[2,2816]{1,0:T(2,128)} %pad_maximum_fusion.63), channel_id=1, source_target_pairs={{0,16},{4,20},{8,24},{12,28},{16,0},{20,4},{24,8},{28,12},{1,17},{... | collective-permute-start | bytes 67592 | tf_op jit(solution)/shard_map/ppermute | solution.py:109
  11.8 56.6 %collective-permute-start.12 = (f32[2,2816]{1,0:T(2,128)}, f32[2,2816]{1,0:T(2,128)}, u32[]{:S(2)}, u32[]{:S(2)}) collective-permute-start(f32[2,2816]{1,0:T(2,128)} %pad_maximum_fusion.63), channel_id=1, source_target_pairs={{0,20},{4,24},{8,28},{12,0},{16,4},{20,8},{24,12},{28,16},{1,21},{... | collective-permute-start | bytes 67592 | tf_op jit(solution)/shard_map/ppermute | solution.py:109
  13.1 56.9 %collective-permute-start.13 = (f32[2,2816]{1,0:T(2,128)}, f32[2,2816]{1,0:T(2,128)}, u32[]{:S(2)}, u32[]{:S(2)}) collective-permute-start(f32[2,2816]{1,0:T(2,128)} %pad_maximum_fusion.63), channel_id=1, source_target_pairs={{0,24},{4,28},{8,0},{12,4},{16,8},{20,12},{24,16},{28,20},{1,25},{... | collective-permute-start | bytes 67592 | tf_op jit(solution)/shard_map/ppermute | solution.py:109
  14.5 56.4 %collective-permute-start.14 = (f32[2,2816]{1,0:T(2,128)}, f32[2,2816]{1,0:T(2,128)}, u32[]{:S(2)}, u32[]{:S(2)}) collective-permute-start(f32[2,2816]{1,0:T(2,128)} %pad_maximum_fusion.63), channel_id=1, source_target_pairs={{0,28},{4,0},{8,4},{12,8},{16,12},{20,16},{24,20},{28,24},{1,29},{... | collective-permute-start | bytes 67592 | tf_op jit(solution)/shard_map/ppermute | solution.py:109
  42.7 28.2 %collective-permute-start.8 = (f32[2,2816]{1,0:T(2,128)}, f32[2,2816]{1,0:T(2,128)S(1)}, u32[]{:S(2)}, u32[]{:S(2)}) collective-permute-start(f32[2,2816]{1,0:T(2,128)} %pad_maximum_fusion.63), channel_id=1, source_target_pairs={{0,4},{4,8},{8,12},{12,16},{16,20},{20,24},{24,28},{28,0},{1,5},{5... | collective-permute-start | bytes 67592 | tf_op jit(solution)/shard_map/ppermute | solution.py:109
  43.4 27.5 %collective-permute-start.9 = (f32[2,2816]{1,0:T(2,128)}, f32[2,2816]{1,0:T(2,128)S(1)}, u32[]{:S(2)}, u32[]{:S(2)}) collective-permute-start(f32[2,2816]{1,0:T(2,128)} %pad_maximum_fusion.63), channel_id=1, source_target_pairs={{0,8},{4,12},{8,16},{12,20},{16,24},{20,28},{24,0},{28,4},{1,9},{5... | collective-permute-start | bytes 67592 | tf_op jit(solution)/shard_map/ppermute | solution.py:109
  92.2 29.1 %collective-permute-start.15 = (bf16[128,1024]{1,0:T(8,128)(2,1)}, bf16[128,1024]{1,0:T(8,128)(2,1)}, u32[]{:S(2)}, u32[]{:S(2)}) collective-permute-start(bf16[128,1024]{1,0:T(8,128)(2,1)} %slice.756), channel_id=1, source_target_pairs={{0,8},{8,16},{16,24},{24,28},{28,20},{20,12},{12,4},{4,0},{1,9},{9... | collective-permute-start | bytes 786440 | tf_op jit(solution)/shard_map/ppermute | solution.py:56
  92.2 29.7 %collective-permute-start.16 = (bf16[128,1024]{1,0:T(8,128)(2,1)}, bf16[128,1024]{1,0:T(8,128)(2,1)}, u32[]{:S(2)}, u32[]{:S(2)}) collective-permute-start(bf16[128,1024]{1,0:T(8,128)(2,1)} %slice.756), channel_id=1, source_target_pairs={{8,0},{16,8},{24,16},{28,24},{20,28},{12,20},{4,12},{0,4},{9,1},{1... | collective-permute-start | bytes 786440 | tf_op jit(solution)/shard_map/ppermute | solution.py:57
  137.2 16.2 %collective-permute-start.23 = (bf16[128,1280]{1,0:T(8,128)(2,1)S(1)}, bf16[128,1280]{1,0:T(8,128)(2,1)S(1)}, u32[]{:S(2)}, u32[]{:S(2)}) collective-permute-start(bf16[128,1280]{1,0:T(8,128)(2,1)S(1)} %copy-done.115), channel_id=1, source_target_pairs={{0,8},{8,16},{16,24},{24,28},{28,20},{20,12},{12,4},{4,0},{1,9},{9... | collective-permute-start | bytes 983048 | tf_op jit(solution)/shard_map/ppermute | solution.py:56
  139.0 16.4 %collective-permute-start.24 = (bf16[128,1280]{1,0:T(8,128)(2,1)S(1)}, bf16[128,1280]{1,0:T(8,128)(2,1)S(1)}, u32[]{:S(2)}, u32[]{:S(2)}) collective-permute-start(bf16[128,1280]{1,0:T(8,128)(2,1)S(1)} %copy-done.115), channel_id=1, source_target_pairs={{8,0},{16,8},{24,16},{28,24},{20,28},{12,20},{4,12},{0,4},{9,1},{1... | collective-permute-start | bytes 983048 | tf_op jit(solution)/shard_map/ppermute | solution.py:57
  171.1 12.5 %collective-permute-start.35 = (bf16[128,768]{1,0:T(8,128)(2,1)S(1)}, bf16[128,768]{1,0:T(8,128)(2,1)S(1)}, u32[]{:S(2)}, u32[]{:S(2)}) collective-permute-start(bf16[128,768]{1,0:T(8,128)(2,1)S(1)} %copy-done.147), channel_id=1, source_target_pairs={{0,8},{8,16},{16,24},{24,28},{28,20},{20,12},{12,4},{4,0},{1,9},{9... | collective-permute-start | bytes 589832 | tf_op jit(solution)/shard_map/ppermute | solution.py:56
  172.0 14.1 %collective-permute-start.36 = (bf16[128,768]{1,0:T(8,128)(2,1)S(1)}, bf16[128,768]{1,0:T(8,128)(2,1)S(1)}, u32[]{:S(2)}, u32[]{:S(2)}) collective-permute-start(bf16[128,768]{1,0:T(8,128)(2,1)S(1)} %copy-done.147), channel_id=1, source_target_pairs={{8,0},{16,8},{24,16},{28,24},{20,28},{12,20},{4,12},{0,4},{9,1},{1... | collective-permute-start | bytes 589832 | tf_op jit(solution)/shard_map/ppermute | solution.py:57
  183.6 21.5 %collective-permute-start.31 = (bf16[256,1024]{1,0:T(8,128)(2,1)S(1)}, bf16[256,1024]{1,0:T(8,128)(2,1)S(1)}, u32[]{:S(2)}, u32[]{:S(2)}) collective-permute-start(bf16[256,1024]{1,0:T(8,128)(2,1)S(1)} %constant_dynamic-slice_fusion.13), channel_id=1, source_target_pairs={{0,1},{1,0},{2,3},{3,2},{4,5},{5,4},{6,7},{7,6},{8,9},{9,8},{10,11... | collective-permute-start | bytes 1572872 | tf_op jit(solution)/shard_map/ppermute | solution.py:129
  199.5 10.1 %collective-permute-start.43 = (bf16[128,1024]{1,0:T(8,128)(2,1)S(1)}, bf16[128,1024]{1,0:T(8,128)(2,1)S(1)}, u32[]{:S(2)}, u32[]{:S(2)}) collective-permute-start(bf16[128,1024]{1,0:T(8,128)(2,1)S(1)} %copy-done.122), channel_id=1, source_target_pairs={{0,8},{8,16},{16,24},{24,28},{28,20},{20,12},{12,4},{4,0},{1,9},{9... | collective-permute-start | bytes 786440 | tf_op jit(solution)/shard_map/ppermute | solution.py:56
  200.3 10.2 %collective-permute-start.44 = (bf16[128,1024]{1,0:T(8,128)(2,1)S(1)}, bf16[128,1024]{1,0:T(8,128)(2,1)S(1)}, u32[]{:S(2)}, u32[]{:S(2)}) collective-permute-start(bf16[128,1024]{1,0:T(8,128)(2,1)S(1)} %copy-done.122), channel_id=1, source_target_pairs={{8,0},{16,8},{24,16},{28,24},{20,28},{12,20},{4,12},{0,4},{9,1},{1... | collective-permute-start | bytes 786440 | tf_op jit(solution)/shard_map/ppermute | solution.py:57
  222.3 19.9 %collective-permute-start.34 = (bf16[256,1024]{1,0:T(8,128)(2,1)S(1)}, bf16[256,1024]{1,0:T(8,128)(2,1)S(1)}, u32[]{:S(2)}, u32[]{:S(2)}) collective-permute-start(bf16[256,1024]{1,0:T(8,128)(2,1)S(1)} %maximum_select_fusion.8), channel_id=1, source_target_pairs={{0,1},{1,0},{2,3},{3,2},{4,5},{5,4},{6,7},{7,6},{8,9},{9,8},{10,11... | collective-permute-start | bytes 1572872 | tf_op jit(solution)/shard_map/ppermute | solution.py:145
  224.7 12.1 %collective-permute-start.51 = (bf16[128,1280]{1,0:T(8,128)(2,1)S(1)}, bf16[128,1280]{1,0:T(8,128)(2,1)}, u32[]{:S(2)}, u32[]{:S(2)}) collective-permute-start(bf16[128,1280]{1,0:T(8,128)(2,1)S(1)} %copy-done.114), channel_id=1, source_target_pairs={{0,8},{8,16},{16,24},{24,28},{28,20},{20,12},{12,4},{4,0},{1,9},{9... | collective-permute-start | bytes 983048 | tf_op jit(solution)/shard_map/ppermute | solution.py:56
  226.1 13.9 %collective-permute-start.52 = (bf16[128,1280]{1,0:T(8,128)(2,1)S(1)}, bf16[128,1280]{1,0:T(8,128)(2,1)}, u32[]{:S(2)}, u32[]{:S(2)}) collective-permute-start(bf16[128,1280]{1,0:T(8,128)(2,1)S(1)} %copy-done.114), channel_id=1, source_target_pairs={{8,0},{16,8},{24,16},{28,24},{20,28},{12,20},{4,12},{0,4},{9,1},{1... | collective-permute-start | bytes 983048 | tf_op jit(solution)/shard_map/ppermute | solution.py:57
  236.7 20.9 %collective-permute-start.53 = (bf16[128,1280]{1,0:T(8,128)(2,1)}, bf16[128,1280]{1,0:T(8,128)(2,1)}, u32[]{:S(2)}, u32[]{:S(2)}) collective-permute-start(bf16[128,1280]{1,0:T(8,128)(2,1)} %collective-permute-done.51), channel_id=1, source_target_pairs={{0,8},{8,16},{16,24},{24,28},{28,20},{20,12},{12,4},{4,0},{1,9},{9... | collective-permute-start | bytes 983048 | tf_op jit(solution)/shard_map/ppermute | solution.py:56
  240.0 20.9 %collective-permute-start.54 = (bf16[128,1280]{1,0:T(8,128)(2,1)}, bf16[128,1280]{1,0:T(8,128)(2,1)}, u32[]{:S(2)}, u32[]{:S(2)}) collective-permute-start(bf16[128,1280]{1,0:T(8,128)(2,1)} %collective-permute-done.52), channel_id=1, source_target_pairs={{8,0},{16,8},{24,16},{28,24},{20,28},{12,20},{4,12},{0,4},{9,1},{1... | collective-permute-start | bytes 983048 | tf_op jit(solution)/shard_map/ppermute | solution.py:57
  312.1 12.1 %collective-permute-start.60 = (bf16[128,1024]{1,0:T(8,128)(2,1)S(1)}, bf16[128,1024]{1,0:T(8,128)(2,1)S(1)}, u32[]{:S(2)}, u32[]{:S(2)}) collective-permute-start(bf16[128,1024]{1,0:T(8,128)(2,1)S(1)} %dynamic-slice_convert_fusion.6), channel_id=1, source_target_pairs={{0,2},{1,3},{2,0},{3,1},{4,6},{5,7},{6,4},{7,5},{8,10},{9,11},{10,... | collective-permute-start | bytes 786440 | tf_op jit(solution)/shard_map/ppermute | solution.py:129
  365.8 10.0 %collective-permute-start.63 = (bf16[256,1024]{1,0:T(8,128)(2,1)}, bf16[256,1024]{1,0:T(8,128)(2,1)}, u32[]{:S(2)}, u32[]{:S(2)}) collective-permute-start(bf16[256,1024]{1,0:T(8,128)(2,1)} %constant_dynamic-slice_fusion.11), channel_id=1, source_target_pairs={{0,1},{1,0},{2,3},{3,2},{4,5},{5,4},{6,7},{7,6},{8,9},{9,8},{10,11... | collective-permute-start | bytes 1572872 | tf_op jit(solution)/shard_map/ppermute | solution.py:129
  377.1 11.0 %collective-permute-start.64 = (bf16[128,1024]{1,0:T(8,128)(2,1)S(1)}, bf16[128,1024]{1,0:T(8,128)(2,1)S(1)}, u32[]{:S(2)}, u32[]{:S(2)}) collective-permute-start(bf16[128,1024]{1,0:T(8,128)(2,1)S(1)} %dynamic-slice_convert_fusion.5), channel_id=1, source_target_pairs={{0,2},{1,3},{2,0},{3,1},{4,6},{5,7},{6,4},{7,5},{8,10},{9,11},{10,... | collective-permute-start | bytes 786440 | tf_op jit(solution)/shard_map/ppermute | solution.py:129
  383.6 15.2 %collective-permute-start.62 = (bf16[256,1024]{1,0:T(8,128)(2,1)S(1)}, bf16[256,1024]{1,0:T(8,128)(2,1)}, u32[]{:S(2)}, u32[]{:S(2)}) collective-permute-start(bf16[256,1024]{1,0:T(8,128)(2,1)S(1)} %maximum_select_fusion.9), channel_id=1, source_target_pairs={{0,1},{1,0},{2,3},{3,2},{4,5},{5,4},{6,7},{7,6},{8,9},{9,8},{10,11... | collective-permute-start | bytes 1572872 | tf_op jit(solution)/shard_map/ppermute | solution.py:145
  390.0 11.5 %collective-permute-start.65 = (bf16[128,1024]{1,0:T(8,128)(2,1)}, bf16[128,1024]{1,0:T(8,128)(2,1)}, u32[]{:S(2)}, u32[]{:S(2)}) collective-permute-start(bf16[128,1024]{1,0:T(8,128)(2,1)} %fusion.117), channel_id=1, source_target_pairs={{0,2},{1,3},{2,0},{3,1},{4,6},{5,7},{6,4},{7,5},{8,10},{9,11},{10,... | collective-permute-start | bytes 786440 | tf_op jit(solution)/shard_map/ppermute | solution.py:145
  489.5 25.3 %collective-permute-start.126 = (f32[2816]{0:T(1024)}, f32[2816]{0:T(1024)}, u32[]{:S(2)}, u32[]{:S(2)}) collective-permute-start(f32[2816]{0:T(1024)} %pad_maximum_fusion.67), channel_id=1, source_target_pairs={{0,4},{4,8},{8,12},{12,16},{16,20},{20,24},{24,28},{28,0},{1,5},{5... | collective-permute-start | bytes 33800 | tf_op jit(solution)/shard_map/ppermute | solution.py:109
  489.9 27.4 %collective-permute-start.127 = (f32[2816]{0:T(1024)}, f32[2816]{0:T(1024)}, u32[]{:S(2)}, u32[]{:S(2)}) collective-permute-start(f32[2816]{0:T(1024)} %pad_maximum_fusion.67), channel_id=1, source_target_pairs={{0,8},{4,12},{8,16},{12,20},{16,24},{20,28},{24,0},{28,4},{1,9},{5... | collective-permute-start | bytes 33800 | tf_op jit(solution)/shard_map/ppermute | solution.py:109
  490.9 28.5 %collective-permute-start.128 = (f32[2816]{0:T(1024)}, f32[2816]{0:T(1024)}, u32[]{:S(2)}, u32[]{:S(2)}) collective-permute-start(f32[2816]{0:T(1024)} %pad_maximum_fusion.67), channel_id=1, source_target_pairs={{0,12},{4,16},{8,20},{12,24},{16,28},{20,0},{24,4},{28,8},{1,13},{... | collective-permute-start | bytes 33800 | tf_op jit(solution)/shard_map/ppermute | solution.py:109
  496.1 14.1 %collective-permute-start.87 = (bf16[128,640]{1,0:T(8,128)(2,1)}, bf16[128,640]{1,0:T(8,128)(2,1)}, u32[]{:S(2)}, u32[]{:S(2)}) collective-permute-start(bf16[128,640]{1,0:T(8,128)(2,1)} %get-tuple-element.135), channel_id=1, source_target_pairs={{0,8},{8,16},{16,24},{24,28},{28,20},{20,12},{12,4},{4,0},{1,9},{9... | collective-permute-start | bytes 491528 | tf_op jit(solution)/shard_map/ppermute | solution.py:81
  499.1 13.1 %collective-permute-start.91 = (bf16[128,640]{1,0:T(8,128)(2,1)}, bf16[128,640]{1,0:T(8,128)(2,1)}, u32[]{:S(2)}, u32[]{:S(2)}) collective-permute-start(bf16[128,640]{1,0:T(8,128)(2,1)} %get-tuple-element.133), channel_id=1, source_target_pairs={{8,0},{16,8},{24,16},{28,24},{20,28},{12,20},{4,12},{0,4},{9,1},{1... | collective-permute-start | bytes 491528 | tf_op jit(solution)/shard_map/ppermute | solution.py:82
  519.4 15.5 %collective-permute-start.67 = (bf16[256,1024]{1,0:T(8,128)(2,1)}, bf16[256,1024]{1,0:T(8,128)(2,1)}, u32[]{:S(2)}, u32[]{:S(2)}) collective-permute-start(bf16[256,1024]{1,0:T(8,128)(2,1)} %constant_dynamic-slice_fusion.10), channel_id=1, source_target_pairs={{0,1},{1,0},{2,3},{3,2},{4,5},{5,4},{6,7},{7,6},{8,9},{9,8},{10,11... | collective-permute-start | bytes 1572872 | tf_op jit(solution)/shard_map/ppermute | solution.py:129
  519.4 17.3 %collective-permute-start.79 = (bf16[256,1024]{1,0:T(8,128)(2,1)}, bf16[256,1024]{1,0:T(8,128)(2,1)S(1)}, u32[]{:S(2)}, u32[]{:S(2)}) collective-permute-start(bf16[256,1024]{1,0:T(8,128)(2,1)} %constant_dynamic-slice_fusion.7), channel_id=1, source_target_pairs={{0,1},{1,0},{2,3},{3,2},{4,5},{5,4},{6,7},{7,6},{8,9},{9,8},{10,11... | collective-permute-start | bytes 1572872 | tf_op jit(solution)/shard_map/ppermute | solution.py:129
  519.9 18.7 %collective-permute-start.75 = (bf16[256,1024]{1,0:T(8,128)(2,1)}, bf16[256,1024]{1,0:T(8,128)(2,1)}, u32[]{:S(2)}, u32[]{:S(2)}) collective-permute-start(bf16[256,1024]{1,0:T(8,128)(2,1)} %constant_dynamic-slice_fusion.8), channel_id=1, source_target_pairs={{0,1},{1,0},{2,3},{3,2},{4,5},{5,4},{6,7},{7,6},{8,9},{9,8},{10,11... | collective-permute-start | bytes 1572872 | tf_op jit(solution)/shard_map/ppermute | solution.py:129
  520.0 10.4 %collective-permute-start.88 = (bf16[128,1280]{1,0:T(8,128)(2,1)}, bf16[128,1280]{1,0:T(8,128)(2,1)}, u32[]{:S(2)}, u32[]{:S(2)}) collective-permute-start(bf16[128,1280]{1,0:T(8,128)(2,1)} %pad_maximum_fusion.33), channel_id=1, source_target_pairs={{0,8},{8,16},{16,24},{24,28},{28,20},{20,12},{12,4},{4,0},{1,9},{9... | collective-permute-start | bytes 983048 | tf_op jit(solution)/shard_map/ppermute | solution.py:98
  521.2 10.1 %collective-permute-start.92 = (bf16[128,1280]{1,0:T(8,128)(2,1)}, bf16[128,1280]{1,0:T(8,128)(2,1)}, u32[]{:S(2)}, u32[]{:S(2)}) collective-permute-start(bf16[128,1280]{1,0:T(8,128)(2,1)} %pad_maximum_fusion.34), channel_id=1, source_target_pairs={{8,0},{16,8},{24,16},{28,24},{20,28},{12,20},{4,12},{0,4},{9,1},{1... | collective-permute-start | bytes 983048 | tf_op jit(solution)/shard_map/ppermute | solution.py:99
  532.7 26.6 %collective-permute-start.89 = (bf16[128,1280]{1,0:T(8,128)(2,1)S(1)}, bf16[128,1280]{1,0:T(8,128)(2,1)S(1)}, u32[]{:S(2)}, u32[]{:S(2)}) collective-permute-start(bf16[128,1280]{1,0:T(8,128)(2,1)S(1)} %get-tuple-element.131), channel_id=1, source_target_pairs={{0,8},{8,16},{16,24},{24,28},{28,20},{20,12},{12,4},{4,0},{1,9},{9... | collective-permute-start | bytes 983048 | tf_op jit(solution)/shard_map/ppermute | solution.py:98
  534.5 24.8 %collective-permute-start.93 = (bf16[128,1280]{1,0:T(8,128)(2,1)S(1)}, bf16[128,1280]{1,0:T(8,128)(2,1)S(1)}, u32[]{:S(2)}, u32[]{:S(2)}) collective-permute-start(bf16[128,1280]{1,0:T(8,128)(2,1)S(1)} %get-tuple-element.130), channel_id=1, source_target_pairs={{8,0},{16,8},{24,16},{28,24},{20,28},{12,20},{4,12},{0,4},{9,1},{1... | collective-permute-start | bytes 983048 | tf_op jit(solution)/shard_map/ppermute | solution.py:99
  536.2 15.1 %collective-permute-start.68 = (bf16[128,1024]{1,0:T(8,128)(2,1)S(1)}, bf16[128,1024]{1,0:T(8,128)(2,1)S(1)}, u32[]{:S(2)}, u32[]{:S(2)}) collective-permute-start(bf16[128,1024]{1,0:T(8,128)(2,1)S(1)} %dynamic-slice_convert_fusion.4), channel_id=1, source_target_pairs={{0,2},{1,3},{2,0},{3,1},{4,6},{5,7},{6,4},{7,5},{8,10},{9,11},{10,... | collective-permute-start | bytes 786440 | tf_op jit(solution)/shard_map/ppermute | solution.py:129
  537.0 14.0 %collective-permute-start.80 = (bf16[128,1024]{1,0:T(8,128)(2,1)S(1)}, bf16[128,1024]{1,0:T(8,128)(2,1)S(1)}, u32[]{:S(2)}, u32[]{:S(2)}) collective-permute-start(bf16[128,1024]{1,0:T(8,128)(2,1)S(1)} %dynamic-slice_convert_fusion.1), channel_id=1, source_target_pairs={{0,2},{1,3},{2,0},{3,1},{4,6},{5,7},{6,4},{7,5},{8,10},{9,11},{10,... | collective-permute-start | bytes 786440 | tf_op jit(solution)/shard_map/ppermute | solution.py:129
  539.9 16.8 %collective-permute-start.76 = (bf16[128,1024]{1,0:T(8,128)(2,1)S(1)}, bf16[128,1024]{1,0:T(8,128)(2,1)S(1)}, u32[]{:S(2)}, u32[]{:S(2)}) collective-permute-start(bf16[128,1024]{1,0:T(8,128)(2,1)S(1)} %dynamic-slice_convert_fusion.2), channel_id=1, source_target_pairs={{0,2},{1,3},{2,0},{3,1},{4,6},{5,7},{6,4},{7,5},{8,10},{9,11},{10,... | collective-permute-start | bytes 786440 | tf_op jit(solution)/shard_map/ppermute | solution.py:129
  557.2 11.1 %collective-permute-start.77 = (bf16[128,1024]{1,0:T(8,128)(2,1)S(1)}, bf16[128,1024]{1,0:T(8,128)(2,1)S(1)}, u32[]{:S(2)}, u32[]{:S(2)}) collective-permute-start(bf16[128,1024]{1,0:T(8,128)(2,1)S(1)} %add_convert_fusion.13), channel_id=1, source_target_pairs={{0,2},{1,3},{2,0},{3,1},{4,6},{5,7},{6,4},{7,5},{8,10},{9,11},{10,... | collective-permute-start | bytes 786440 | tf_op jit(solution)/shard_map/ppermute | solution.py:145
  557.8 13.6 %collective-permute-start.69 = (bf16[128,1024]{1,0:T(8,128)(2,1)S(1)}, bf16[128,1024]{1,0:T(8,128)(2,1)S(1)}, u32[]{:S(2)}, u32[]{:S(2)}) collective-permute-start(bf16[128,1024]{1,0:T(8,128)(2,1)S(1)} %get-tuple-element.158), channel_id=1, source_target_pairs={{0,2},{1,3},{2,0},{3,1},{4,6},{5,7},{6,4},{7,5},{8,10},{9,11},{10,... | collective-permute-start | bytes 786440 | tf_op jit(solution)/shard_map/ppermute | solution.py:145
  560.6 11.7 %collective-permute-start.90 = (bf16[128,1280]{1,0:T(8,128)(2,1)S(1)}, bf16[128,1280]{1,0:T(8,128)(2,1)S(1)}, u32[]{:S(2)}, u32[]{:S(2)}) collective-permute-start(bf16[128,1280]{1,0:T(8,128)(2,1)S(1)} %get-tuple-element.129), channel_id=1, source_target_pairs={{0,8},{8,16},{16,24},{24,28},{28,20},{20,12},{12,4},{4,0},{1,9},{9... | collective-permute-start | bytes 983048 | tf_op jit(solution)/shard_map/ppermute | solution.py:98
  562.8 22.4 %collective-permute-start.82 = (bf16[256,1024]{1,0:T(8,128)(2,1)S(1)}, bf16[256,1024]{1,0:T(8,128)(2,1)S(1)}, u32[]{:S(2)}, u32[]{:S(2)}) collective-permute-start(bf16[256,1024]{1,0:T(8,128)(2,1)S(1)} %maximum_select_fusion.14), channel_id=1, source_target_pairs={{0,1},{1,0},{2,3},{3,2},{4,5},{5,4},{6,7},{7,6},{8,9},{9,8},{10,11... | collective-permute-start | bytes 1572872 | tf_op jit(solution)/shard_map/ppermute | solution.py:145
  569.3 59.4 %collective-permute-start.78 = (bf16[256,1024]{1,0:T(8,128)(2,1)}, bf16[256,1024]{1,0:T(8,128)(2,1)}, u32[]{:S(2)}, u32[]{:S(2)}) collective-permute-start(bf16[256,1024]{1,0:T(8,128)(2,1)} %maximum_select_fusion.13), channel_id=1, source_target_pairs={{0,1},{1,0},{2,3},{3,2},{4,5},{5,4},{6,7},{7,6},{8,9},{9,8},{10,11... | collective-permute-start | bytes 1572872 | tf_op jit(solution)/shard_map/ppermute | solution.py:145
  572.3 61.3 %collective-permute-start.70 = (bf16[256,1024]{1,0:T(8,128)(2,1)}, bf16[256,1024]{1,0:T(8,128)(2,1)}, u32[]{:S(2)}, u32[]{:S(2)}) collective-permute-start(bf16[256,1024]{1,0:T(8,128)(2,1)} %maximum_select_fusion.11), channel_id=1, source_target_pairs={{0,1},{1,0},{2,3},{3,2},{4,5},{5,4},{6,7},{7,6},{8,9},{9,8},{10,11... | collective-permute-start | bytes 1572872 | tf_op jit(solution)/shard_map/ppermute | solution.py:145
  582.4 57.0 %collective-permute-start.100 = (bf16[128,1792]{1,0:T(8,128)(2,1)}, bf16[128,1792]{1,0:T(8,128)(2,1)}, u32[]{:S(2)}, u32[]{:S(2)}) collective-permute-start(bf16[128,1792]{1,0:T(8,128)(2,1)} %pad_maximum_fusion.28), channel_id=1, source_target_pairs={{8,0},{16,8},{24,16},{28,24},{20,28},{12,20},{4,12},{0,4},{9,1},{1... | collective-permute-start | bytes 1376264 | tf_op jit(solution)/shard_map/ppermute | solution.py:99
  583.5 56.0 %collective-permute-start.96 = (bf16[128,1792]{1,0:T(8,128)(2,1)}, bf16[128,1792]{1,0:T(8,128)(2,1)}, u32[]{:S(2)}, u32[]{:S(2)}) collective-permute-start(bf16[128,1792]{1,0:T(8,128)(2,1)} %pad_maximum_fusion.27), channel_id=1, source_target_pairs={{0,8},{8,16},{16,24},{24,28},{28,20},{20,12},{12,4},{4,0},{1,9},{9... | collective-permute-start | bytes 1376264 | tf_op jit(solution)/shard_map/ppermute | solution.py:98
  623.8 31.5 %collective-permute-start.119 = (f32[2816]{0:T(1024)S(1)}, f32[2816]{0:T(1024)S(1)}, u32[]{:S(2)}, u32[]{:S(2)}) collective-permute-start(f32[2816]{0:T(1024)S(1)} %pad_maximum_fusion.66), channel_id=1, source_target_pairs={{0,4},{4,8},{8,12},{12,16},{16,20},{20,24},{24,28},{28,0},{1,5},{5... | collective-permute-start | bytes 33800 | tf_op jit(solution)/shard_map/ppermute | solution.py:109
  628.6 27.7 %collective-permute-start.120 = (f32[2816]{0:T(1024)S(1)}, f32[2816]{0:T(1024)S(1)}, u32[]{:S(2)}, u32[]{:S(2)}) collective-permute-start(f32[2816]{0:T(1024)S(1)} %pad_maximum_fusion.66), channel_id=1, source_target_pairs={{0,8},{4,12},{8,16},{12,20},{16,24},{20,28},{24,0},{28,4},{1,9},{5... | collective-permute-start | bytes 33800 | tf_op jit(solution)/shard_map/ppermute | solution.py:109
  633.6 24.4 %collective-permute-start.121 = (f32[2816]{0:T(1024)S(1)}, f32[2816]{0:T(1024)S(1)}, u32[]{:S(2)}, u32[]{:S(2)}) collective-permute-start(f32[2816]{0:T(1024)S(1)} %pad_maximum_fusion.66), channel_id=1, source_target_pairs={{0,12},{4,16},{8,20},{12,24},{16,28},{20,0},{24,4},{28,8},{1,13},{... | collective-permute-start | bytes 33800 | tf_op jit(solution)/shard_map/ppermute | solution.py:109
  642.1 10.4 %collective-permute-start.101 = (bf16[128,1792]{1,0:T(8,128)(2,1)S(1)}, bf16[128,1792]{1,0:T(8,128)(2,1)S(1)}, u32[]{:S(2)}, u32[]{:S(2)}) collective-permute-start(bf16[128,1792]{1,0:T(8,128)(2,1)S(1)} %get-tuple-element.111), channel_id=1, source_target_pairs={{8,0},{16,8},{24,16},{28,24},{20,28},{12,20},{4,12},{0,4},{9,1},{1... | collective-permute-start | bytes 1376264 | tf_op jit(solution)/shard_map/ppermute | solution.py:99
  643.0 12.1 %collective-permute-start.97 = (bf16[128,1792]{1,0:T(8,128)(2,1)S(1)}, bf16[128,1792]{1,0:T(8,128)(2,1)S(1)}, u32[]{:S(2)}, u32[]{:S(2)}) collective-permute-start(bf16[128,1792]{1,0:T(8,128)(2,1)S(1)} %get-tuple-element.110), channel_id=1, source_target_pairs={{0,8},{8,16},{16,24},{24,28},{28,20},{20,12},{12,4},{4,0},{1,9},{9... | collective-permute-start | bytes 1376264 | tf_op jit(solution)/shard_map/ppermute | solution.py:98
  655.1 17.8 %collective-permute-start.83 = (bf16[256,1024]{1,0:T(8,128)(2,1)S(1)}, bf16[256,1024]{1,0:T(8,128)(2,1)S(1)}, u32[]{:S(2)}, u32[]{:S(2)}) collective-permute-start(bf16[256,1024]{1,0:T(8,128)(2,1)S(1)} %constant_dynamic-slice_fusion.6), channel_id=1, source_target_pairs={{0,1},{1,0},{2,3},{3,2},{4,5},{5,4},{6,7},{7,6},{8,9},{9,8},{10,11... | collective-permute-start | bytes 1572872 | tf_op jit(solution)/shard_map/ppermute | solution.py:129
  656.3 14.3 %collective-permute-start.102 = (bf16[128,1792]{1,0:T(8,128)(2,1)S(1)}, bf16[128,1792]{1,0:T(8,128)(2,1)S(1)}, u32[]{:S(2)}, u32[]{:S(2)}) collective-permute-start(bf16[128,1792]{1,0:T(8,128)(2,1)S(1)} %get-tuple-element.109), channel_id=1, source_target_pairs={{8,0},{16,8},{24,16},{28,24},{20,28},{12,20},{4,12},{0,4},{9,1},{1... | collective-permute-start | bytes 1376264 | tf_op jit(solution)/shard_map/ppermute | solution.py:99
  658.0 12.7 %collective-permute-start.98 = (bf16[128,1792]{1,0:T(8,128)(2,1)S(1)}, bf16[128,1792]{1,0:T(8,128)(2,1)S(1)}, u32[]{:S(2)}, u32[]{:S(2)}) collective-permute-start(bf16[128,1792]{1,0:T(8,128)(2,1)S(1)} %get-tuple-element.108), channel_id=1, source_target_pairs={{0,8},{8,16},{16,24},{24,28},{28,20},{20,12},{12,4},{4,0},{1,9},{9... | collective-permute-start | bytes 1376264 | tf_op jit(solution)/shard_map/ppermute | solution.py:98
  659.3 10.2 %collective-permute-start.124 = (f32[2816]{0:T(1024)S(1)}, f32[2816]{0:T(1024)S(1)}, u32[]{:S(2)}, u32[]{:S(2)}) collective-permute-start(f32[2816]{0:T(1024)S(1)} %pad_maximum_fusion.66), channel_id=1, source_target_pairs={{0,24},{4,28},{8,0},{12,4},{16,8},{20,12},{24,16},{28,20},{1,25},{... | collective-permute-start | bytes 33800 | tf_op jit(solution)/shard_map/ppermute | solution.py:109
  691.9 10.3 %collective-permute-start.85 = (bf16[128,1024]{1,0:T(8,128)(2,1)S(1)}, bf16[128,1024]{1,0:T(8,128)(2,1)S(1)}, u32[]{:S(2)}, u32[]{:S(2)}) collective-permute-start(bf16[128,1024]{1,0:T(8,128)(2,1)S(1)} %add_convert_fusion.12), channel_id=1, source_target_pairs={{0,2},{1,3},{2,0},{3,1},{4,6},{5,7},{6,4},{7,5},{8,10},{9,11},{10,... | collective-permute-start | bytes 786440 | tf_op jit(solution)/shard_map/ppermute | solution.py:145
  702.3 18.9 %collective-permute-start.86 = (bf16[256,1024]{1,0:T(8,128)(2,1)S(1)}, bf16[256,1024]{1,0:T(8,128)(2,1)S(1)}, u32[]{:S(2)}, u32[]{:S(2)}) collective-permute-start(bf16[256,1024]{1,0:T(8,128)(2,1)S(1)} %maximum_select_fusion.15), channel_id=1, source_target_pairs={{0,1},{1,0},{2,3},{3,2},{4,5},{5,4},{6,7},{7,6},{8,9},{9,8},{10,11... | collective-permute-start | bytes 1572872 | tf_op jit(solution)/shard_map/ppermute | solution.py:145
  718.8 11.0 %collective-permute-start.116 = (bf16[128,1792]{1,0:T(8,128)(2,1)S(1)}, bf16[128,1792]{1,0:T(8,128)(2,1)S(1)}, u32[]{:S(2)}, u32[]{:S(2)}) collective-permute-start(bf16[128,1792]{1,0:T(8,128)(2,1)S(1)} %pad_maximum_fusion.30), channel_id=1, source_target_pairs={{8,0},{16,8},{24,16},{28,24},{20,28},{12,20},{4,12},{0,4},{9,1},{1... | collective-permute-start | bytes 1376264 | tf_op jit(solution)/shard_map/ppermute | solution.py:99
  718.9 12.9 %collective-permute-start.112 = (bf16[128,1792]{1,0:T(8,128)(2,1)S(1)}, bf16[128,1792]{1,0:T(8,128)(2,1)S(1)}, u32[]{:S(2)}, u32[]{:S(2)}) collective-permute-start(bf16[128,1792]{1,0:T(8,128)(2,1)S(1)} %pad_maximum_fusion.29), channel_id=1, source_target_pairs={{0,8},{8,16},{16,24},{24,28},{28,20},{20,12},{12,4},{4,0},{1,9},{9... | collective-permute-start | bytes 1376264 | tf_op jit(solution)/shard_map/ppermute | solution.py:98
  732.0 12.8 %collective-permute-start.113 = (bf16[128,1792]{1,0:T(8,128)(2,1)S(1)}, bf16[128,1792]{1,0:T(8,128)(2,1)S(1)}, u32[]{:S(2)}, u32[]{:S(2)}) collective-permute-start(bf16[128,1792]{1,0:T(8,128)(2,1)S(1)} %get-tuple-element.100), channel_id=1, source_target_pairs={{0,8},{8,16},{16,24},{24,28},{28,20},{20,12},{12,4},{4,0},{1,9},{9... | collective-permute-start | bytes 1376264 | tf_op jit(solution)/shard_map/ppermute | solution.py:98
  734.3 13.3 %collective-permute-start.117 = (bf16[128,1792]{1,0:T(8,128)(2,1)S(1)}, bf16[128,1792]{1,0:T(8,128)(2,1)S(1)}, u32[]{:S(2)}, u32[]{:S(2)}) collective-permute-start(bf16[128,1792]{1,0:T(8,128)(2,1)S(1)} %get-tuple-element.101), channel_id=1, source_target_pairs={{8,0},{16,8},{24,16},{28,24},{20,28},{12,20},{4,12},{0,4},{9,1},{1... | collective-permute-start | bytes 1376264 | tf_op jit(solution)/shard_map/ppermute | solution.py:99
  (299 other events, 2464.6 us)
